TPU v7x, 512 devices: a whole 4x4x16 slice. The times are simulated.
512 devices in a mesh: beam: 16 (over y, x), ma: 32 (over z, core).
Axes of the slice: x: 4, y: 4, z: 16, core: 2. Of those that a mesh axis runs over, the one named last changes fastest.
Arguments:
- sky_harmonics: float32 [64, 2, 2048], P('ma'), may hold values from -6 to 6
- beam_harmonics: float32 [128, 2, 2048], P('beam'), may hold values from -6 to 6
- wigner: bfloat16 [128, 64, 64, 2048], P('beam', 'ma'), may hold values from -0.125 to 0.125
- order_map: int32 [64], replicated, may hold values from 0 to 2047, as said below
- block_owner: int32 [4096, 1], P('ma'), may hold values from 0 to 31; in each aligned block of 128 rows (0 to 127, 128 to 255, ...) at most 8 rows name the same one
- block_local: int32 [4096], P('ma'), may hold values from 0 to 63
- cell_offset: int32 [524288], P('ma'), may hold values from 0 to 126
- cell_fraction: float32 [524288], P('ma'), may hold values from 0 to 1
- beam_angle: float32 [524288], P('ma'), may hold values from -3.140625 to 3.140625
- sample_count: int32 [32], P('ma'), may hold values from 1 to 16384, 393216 in all
- noise_weight: float32 [128, 128], replicated, may hold values from -0.2 to 2, as said below
Outputs:
- sky_gradient: float32 [64, 2, 2048], P('ma', None, 'beam')
Inputs may be any that keep to these rules, and one draw needn't show every extreme that they name: `order_map`: 64 distinct azimuthal orders. `block_owner`: among the 128 sample blocks of one device, at most 8 name the same owner, and in some device some owner is named exactly 8 times. `noise_weight`: diagonal entries lie in 1 to 2, the others within 0.2 in magnitude.
All inputs are finite; a program needn't handle non-finite values. No bound on the sum of `sample_count` on one device may be relied on, other than what follows from the above.
Results may differ from a plain program's by a relative error of at most 0.017.
Values may be sent and summed in bfloat16 or wider, within the bound.
A program may use at most 128 MiB of HBM per device.

v0:
```python
import math

import jax
import jax.numpy as jnp
from jax import lax
from jax.sharding import PartitionSpec as P

PHI = 4096
CELLS = 128


def copy_for_each(array, axis):
    devices = lax.axis_size(axis)
    return lax.all_to_all(
        jnp.broadcast_to(array[None], (devices, *array.shape)), axis, 0, 0, tiled=True
    )


def of_everyone(array, axis):
    return copy_for_each(array, axis).astype(jnp.float32).sum(axis=0)


def split_up(array, dim, devices):
    shape = array.shape
    blocks = array.reshape(*shape[:dim], devices, shape[dim] // devices, *shape[dim + 1 :])
    return jnp.moveaxis(blocks, dim, 0)


def summed_on_arrival(array, axis, dim):
    blocks = split_up(array, dim, lax.axis_size(axis))
    arrived = lax.all_to_all(blocks, axis, split_axis=0, concat_axis=0, tiled=True)
    return arrived.astype(jnp.float32).sum(axis=0)


def cycle_phases(order_map, cycle_cells):
    stepped = jnp.arange(cycle_cells, dtype=jnp.int32)
    phase_turns = order_map[:, None] * stepped[None, :] % cycle_cells
    angles = phase_turns.astype(jnp.float32) * (2.0 * math.pi / cycle_cells)
    scaling = 1.0 / math.sqrt(order_map.shape[0])
    return jnp.stack([jnp.cos(angles), -jnp.sin(angles)], axis=1) * scaling


def rotation(beam_order, beam_angle, total_orders):
    spin_order = ((beam_order + 1) // 2).astype(jnp.float32)
    angles = spin_order * beam_angle
    return jnp.where(beam_order % 2 == 0, jnp.cos(angles), jnp.sin(angles)) / math.sqrt(
        total_orders
    )


def harmonic_product(sky_harmonics, beam_harmonics):
    sky_real = sky_harmonics[None, :, 0]
    sky_imag = sky_harmonics[None, :, 1]
    beam_real = beam_harmonics[:, None, 0]
    beam_imag = beam_harmonics[:, None, 1]
    first = sky_real * beam_real - sky_imag * beam_imag
    second = sky_real * beam_imag + sky_imag * beam_real
    return jnp.stack([first, second], axis=2).astype(jnp.bfloat16)


def gradient_terms(grad_harmonics, beam_harmonics):
    grad_real = grad_harmonics[:, :, 0]
    grad_imag = grad_harmonics[:, :, 1]
    beam_real = beam_harmonics[:, None, 0]
    beam_imag = beam_harmonics[:, None, 1]
    first = jnp.sum(grad_real * beam_real + grad_imag * beam_imag, axis=0)
    second = jnp.sum(grad_imag * beam_real - grad_real * beam_imag, axis=0)
    return jnp.stack([first, second], axis=1)


def interpolate(flat_values, flat_low, fractions):
    return (1.0 - fractions) * flat_values[:, flat_low] + fractions * flat_values[:, flat_low + 1]


def spread(weighted, flat_low, fractions, span_cells):
    blank_grid = jnp.zeros((weighted.shape[0], span_cells), jnp.float32)
    blank_grid = blank_grid.at[:, flat_low].add((1.0 - fractions) * weighted)
    return blank_grid.at[:, flat_low + 1].add(fractions * weighted)


def local(
    sky_harmonics,
    beam_harmonics,
    wigner,
    order_map,
    block_owner,
    block_local,
    cell_offset,
    cell_fraction,
    beam_angle,
    sample_count,
    noise_weight,
):
    highest = lax.Precision.HIGHEST
    ma_count = lax.axis_size("ma")
    beam_count = lax.axis_size("beam")
    local_orders = beam_harmonics.shape[0]
    total_orders = local_orders * beam_count
    cycle_cells = PHI
    block_cells = CELLS
    sample_blocks = block_owner.shape[0]
    capacity = 2 * sample_blocks // ma_count
    cycle_count = wigner.shape[2]
    cycles_local = cycle_count // ma_count
    blocks_local = cycles_local * cycle_cells // block_cells
    product = harmonic_product(sky_harmonics, beam_harmonics)
    cycle_modes = jnp.einsum("kmcl,kmrl->kmcr", product, wigner, preferred_element_type=jnp.float32)
    slab_modes = lax.all_to_all(cycle_modes, "ma", split_axis=3, concat_axis=1, tiled=True)
    phase_table = cycle_phases(order_map, cycle_cells)
    cycle_cube = jnp.einsum("kmcr,mcp->krp", slab_modes, phase_table, precision=highest)
    owners = block_owner[:, 0]
    owner_hot = (owners[:, None] == jnp.arange(ma_count, dtype=jnp.int32)[None, :]).astype(
        jnp.int32
    )
    slot_rank = jnp.sum((jnp.cumsum(owner_hot, axis=0) - owner_hot) * owner_hot, axis=1)
    slot_index = owners * capacity + slot_rank
    requests = jnp.full((ma_count * capacity,), -1, jnp.int32).at[slot_index].set(block_local)
    requests = requests.reshape(ma_count, capacity)
    offsets = cell_offset.reshape(sample_blocks, block_cells)
    fractions = cell_fraction.reshape(sample_blocks, block_cells)
    angles = beam_angle.reshape(sample_blocks, block_cells)
    beam_order = lax.axis_index("beam") * local_orders + jnp.arange(local_orders, dtype=jnp.int32)
    stamps = jnp.arange(sample_blocks * block_cells, dtype=jnp.int32).reshape(
        sample_blocks, block_cells
    )
    valid_mask = (stamps < sample_count[0]).astype(jnp.float32)
    wanted = lax.all_to_all(requests, "ma", split_axis=0, concat_axis=0, tiled=True)
    wanted_flat = wanted.reshape(-1)
    outgoing = jnp.take(
        cycle_cube.reshape(local_orders, blocks_local, block_cells),
        jnp.clip(wanted_flat, 0, blocks_local - 1),
        axis=1,
    )
    outgoing = outgoing * (wanted_flat >= 0).astype(jnp.float32)[None, :, None]
    incoming = lax.all_to_all(
        outgoing.reshape(local_orders, ma_count, capacity, block_cells).astype(jnp.bfloat16),
        "ma",
        split_axis=1,
        concat_axis=1,
        tiled=True,
    ).astype(jnp.float32)
    blocks = jnp.take(
        incoming.reshape(local_orders, ma_count * capacity, block_cells), slot_index, axis=1
    )
    own_low = jnp.arange(sample_blocks, dtype=jnp.int32)[:, None] * block_cells + offsets
    own_turn = rotation(beam_order[:, None, None], angles[None], total_orders)
    values = interpolate(
        blocks.reshape(local_orders, sample_blocks * block_cells), own_low, fractions
    )
    partial_value = jnp.sum(own_turn * values, axis=0)
    signal = (
        of_everyone(partial_value.astype(jnp.bfloat16), "beam").astype(jnp.float32) * valid_mask
    )
    filtered = jnp.einsum("bu,tu->bt", signal, noise_weight, precision=highest) * valid_mask
    weighted = own_turn * filtered[None]
    own_spread = spread(weighted, own_low, fractions, sample_blocks * block_cells)
    own_spread = own_spread.reshape(local_orders, sample_blocks, block_cells)
    back_slots = (
        jnp.zeros((local_orders, ma_count * capacity, block_cells), jnp.float32)
        .at[:, slot_index]
        .set(own_spread)
    )
    arrived = lax.all_to_all(
        back_slots.reshape(local_orders, ma_count, capacity, block_cells).astype(jnp.bfloat16),
        "ma",
        split_axis=1,
        concat_axis=1,
        tiled=True,
    ).astype(jnp.float32)
    chooser = (wanted_flat[None, :] == jnp.arange(blocks_local, dtype=jnp.int32)[:, None]).astype(
        jnp.float32
    )
    cube_grad = jnp.einsum(
        "gs,ksc->kgc",
        chooser,
        arrived.reshape(local_orders, ma_count * capacity, block_cells),
        precision=highest,
    )
    cube_grad = cube_grad.reshape(local_orders, cycles_local, cycle_cells)
    grad_modes = jnp.einsum("krp,mcp->kmcr", cube_grad, phase_table, precision=highest).astype(
        jnp.bfloat16
    )
    grad_cycles = lax.all_to_all(grad_modes, "ma", split_axis=1, concat_axis=3, tiled=True)
    grad_harmonics = jnp.einsum(
        "kmcr,kmrl->kmcl", grad_cycles, wigner, preferred_element_type=jnp.float32
    )
    gradient = gradient_terms(grad_harmonics, beam_harmonics)
    result = summed_on_arrival(gradient.astype(jnp.bfloat16), "beam", 2)
    return result


def solution(mesh):
    return jax.shard_map(
        local,
        mesh=mesh,
        in_specs=(
            P("ma", None, None),
            P("beam", None, None),
            P("beam", "ma", None, None),
            P(),
            P("ma", None),
            P("ma"),
            P("ma"),
            P("ma"),
            P("ma"),
            P("ma"),
            P(),
        ),
        out_specs=P("ma", None, "beam"),
        check_vma=False,
    )
```

profile of v0, /device:TPU:1, one launch (start us, length us, event | category | flops | bytes accessed | tf_op | source)
XLA Modules:
  0.0 597.0 jit_solution(5402851796727341372)
XLA Ops:
  1.8 1.2 and_bitcast_fusion
  4.8 16.7 %all-to-all-start = ((s32[32,1,8]{2,1,0:T(1,128)}), s32[32,1,8]{2,1,0:T(1,128)S(1)}, u32[]{:S(2)}, u32[]{:S(2)}) async-start(s32[32,1,8]{2,1,0:T(1,128)} %bitcast.12), calls=%async_computation | async-start | bytes 32768 | tf_op jit(solution)/shard_map/all_to_all | solution.py:127
  23.5 4.8 fusion.31
  28.7 3.4 fusion.34
  33.3 11.7 %all-to-all-start.1 = ((f32[8,2,2,64]{0,2,1,3:T(2,128)}), f32[8,2,2,64]{0,2,1,3:T(2,128)S(1)}, u32[]{:S(2)}, u32[]{:S(2)}) async-start(f32[8,2,2,64]{0,2,1,3:T(2,128)} %copy.89), calls=%async_computation.1 | async-start | bytes 262144 | tf_op jit(solution)/shard_map/all_to_all | solution.py:108
  45.6 1.3 fusion.65
  48.2 12.7 %all-to-all-done.1 = f32[8,2,2,64]{0,2,1,3:T(2,128)S(1)} async-done(((f32[8,2,2,64]{0,2,1,3:T(2,128)}), f32[8,2,2,64]{0,2,1,3:T(2,128)S(1)}, u32[]{:S(2)}, u32[]{:S(2)}) %all-to-all-start.1) | async-done | bytes 8224 | tf_op jit(solution)/shard_map/all_to_all | solution.py:108
  61.0 1.2 fusion.12
  62.2 1.2 gather_fusion
  63.4 2.1 multiply_convert_fusion
  65.4 5.8 all-to-all-start.2
  72.6 1.6 broadcast_clamp_fusion
  74.2 30.6 %all-to-all-done.2 = bf16[8,32,8,128]{3,0,2,1:T(8,128)(2,1)} async-done(((bf16[8,32,8,128]{3,0,2,1:T(8,128)(2,1)}), bf16[8,32,8,128]{3,0,2,1:T(8,128)(2,1)}, u32[]{:S(2)}, u32[]{:S(2)}) %all-to-all-start.2) | async-done | bytes 524320 | tf_op jit(solution)/shard_map/all_to_all | solution.py:135
  105.9 1.5 gather_fusion.1
  107.5 5.7 copy.95
  113.1 13.1 %broadcast_select_fusion = f32[8,16384]{0,1:T(8,128)} fusion(f32[8,16384]{0,1:T(8,128)} %copy.95, pred[16384]{0:T(1024)(128)(4,1)S(1)} %broadcast_bitcast_fusion), kind=kLoop, calls=%fused_computation.17 | loop fusion | flops 131072 | bytes 1064960 | tf_op jit(solution)/shard_map/jit(_take)/select_n | solution.py:142
  126.2 57.8 %gather_fusion.2 = f32[16384,8]{1,0:T(8,128)} fusion(f32[8,16384]{0,1:T(8,128)} %broadcast_select_fusion, s32[16384]{0:T(1024)S(1)} %copy-done.7), kind=kCustom, calls=%fused_computation.2 | custom fusion | bytes 1114112 | tf_op jit(solution)/shard_map/gather | solution.py:72
  184.0 57.8 %gather_fusion.3 = f32[16384,8]{1,0:T(8,128)} fusion(f32[8,16384]{0,1:T(8,128)} %broadcast_select_fusion, s32[16384]{0:T(1024)S(1)} %get-tuple-element.11), kind=kCustom, calls=%fused_computation.3 | custom fusion | bytes 1114112 | tf_op jit(solution)/shard_map/gather | solution.py:72
  241.8 39.0 %fusion.6 = bf16[128,128]{1,0:T(8,128)(2,1)S(1)} fusion(f32[128,128,8]{2,1,0:T(8,128)} %bitcast.131, f32[128,128,8]{2,1,0:T(8,128)} %bitcast.130, f32[128,128]{1,0:T(8,128)S(1)} %bitcast.138, f32[128,128]{1,0:T(8,128)S(1)} %broadcast_subtract_fusion, f32[128,128]{1,0:T(8,128)S(1)} %bitcast.142, f32[8]{0:T(128)S(1)} %fusion.56, pred[8]{0:T(512)(128)(4,1)S(1)} %fusion.52), kind=kLoop, calls=%fused_computation.16 | loop fusion | flops 1032192 | bytes 1277992 | tf_op jit(solution)/shard_map/reduce_sum | solution.py:150
  281.7 6.8 %all-to-all-start.3 = ((bf16[16,128,128]{2,1,0:T(8,128)(2,1)}), bf16[16,128,128]{2,1,0:T(8,128)(2,1)S(1)}, u32[]{:S(2)}, u32[]{:S(2)}) async-start(bf16[16,128,128]{2,1,0:T(8,128)(2,1)} %broadcast_in_dim.73), calls=%async_computation.3 | async-start | bytes 1048576 | tf_op jit(solution)/shard_map/all_to_all | solution.py:14
  289.1 10.0 %all-to-all-done.3 = bf16[16,128,128]{2,1,0:T(8,128)(2,1)S(1)} async-done(((bf16[16,128,128]{2,1,0:T(8,128)(2,1)}), bf16[16,128,128]{2,1,0:T(8,128)(2,1)S(1)}, u32[]{:S(2)}, u32[]{:S(2)}) %all-to-all-start.3) | async-done | bytes 524320 | tf_op jit(solution)/shard_map/all_to_all | solution.py:14
  299.4 33.4 %fusion.3 = (f32[8,128,128]{0,2,1:T(8,128)}, f32[8,128,128]{0,2,1:T(8,128)}) fusion(f32[128,128]{1,0:T(8,128)S(1)} %fusion.14, f32[128,128]{1,0:T(8,128)S(1)} %bitcast.139, f32[128,128]{1,0:T(8,128)S(1)} %bitcast.143, f32[8]{0:T(128)S(1)} %fusion.56, pred[8]{0:T(512)(128)(4,1)S(1)} %fusion.52, f32[128,128]{1,0:T(8,128)S(1)} %broadcast_subtract_fusion), kind=kLoop, calls=%fused_computation.13 | loop fusion | flops 655360 | bytes 1310760 | tf_op jit(solution)/shard_map/mul | solution.py:78
  332.8 91.3 %scatter_custom_fusion.1 = f32[8,16384]{0,1:T(8,128)} fusion(s32[16384]{0:T(1024)} %get-tuple-element.24, f32[16384,8]{1,0:T(8,128)} %bitcast.132, f32[]{:T(128)} %constant.97.clone.1), kind=kCustom, calls=%fused_computation.18 | custom fusion | flops 131072 | bytes 524800 | tf_op jit(solution)/shard_map/scatter-add | solution.py:77
  424.1 85.3 %scatter_fusion = f32[8,16384]{0,1:T(8,128)} fusion(f32[8,16384]{0,1:T(8,128)} %scatter_custom_fusion.1, s32[16384]{0:T(1024)S(1)} %get-tuple-element.12, f32[16384,8]{1,0:T(8,128)} %bitcast.129), kind=kCustom, calls=%fused_computation.6 | custom fusion | flops 131072 | bytes 1638400 | tf_op jit(solution)/shard_map/scatter-add | solution.py:78
  509.4 5.9 copy.96
  515.4 8.7 %scatter_fusion.1 = f32[8,256,128]{2,0,1:T(8,128)S(1)} fusion(f32[8,256,128]{2,0,1:T(8,128)S(1)} %broadcast_in_dim.40, s32[128]{0:T(128)S(1)} %bitcast.154, f32[128,8,128]{2,1,0:T(8,128)} %bitcast.135), kind=kCustom, calls=%fused_computation.7 | custom fusion | bytes 1573376 | tf_op jit(solution)/shard_map/scatter | solution.py:161
  525.1 5.6 all-to-all-start.4
  530.8 33.4 %all-to-all-done.4 = bf16[8,32,8,128]{3,2,0,1:T(8,128)(2,1)S(1)} async-done(((bf16[8,32,8,128]{3,2,0,1:T(8,128)(2,1)}), bf16[8,32,8,128]{3,2,0,1:T(8,128)(2,1)S(1)}, u32[]{:S(2)}, u32[]{:S(2)}) %all-to-all-start.4) | async-done | bytes 524320 | tf_op jit(solution)/shard_map/all_to_all | solution.py:163
  564.6 2.5 fusion.18
  567.3 16.4 %all_to_all.65 = bf16[8,64,2,2]{0,3,2,1:T(2,128)(2,1)S(1)} all-to-all(bf16[8,64,2,2]{0,3,2,1:T(2,128)(2,1)S(1)} %copy.100), channel_id=1, replica_groups=mesh['beam'=16,'ma'=32] {'ma'}, dimensions={1} | all-to-all | bytes 8192 | tf_op jit(solution)/shard_map/all_to_all | solution.py:183
  583.9 2.8 fusion.71
  587.3 9.1 %all_to_all.66 = bf16[16,2,2,128]{3,1,2,0:T(2,128)(2,1)S(1)} all-to-all(bf16[16,2,2,128]{3,1,2,0:T(2,128)(2,1)S(1)} %maximum_bitcast_fusion), channel_id=1, replica_groups=mesh['beam'=16,'ma'=32] {'beam'}, dimensions={0} | all-to-all | bytes 32768 | tf_op jit(solution)/shard_map/all_to_all | solution.py:31
  (67 shorter events, 15.7 us)
Async XLA Ops:
  0.0 299.1 %copy-start = (f32[128,128]{1,0:T(8,128)S(1)}, f32[128,128]{1,0:T(8,128)}, u32[]{:S(2)}) copy-start(f32[128,128]{1,0:T(8,128)} %param.21) | copy-start | bytes 196612
  0.0 71.9 %copy-start.1 = (f32[16384]{0:T(1024)S(1)}, f32[16384]{0:T(1024)}, u32[]{:S(2)}) copy-start(f32[16384]{0:T(1024)} %param.18) | copy-start | bytes 196612
  3.0 19.7 %copy-start.9 = (s32[128,1]{0,1:T(1,128)}, s32[128,1]{0,1:T(1,128)S(1)}, u32[]{:S(2)}) copy-start(s32[128,1]{0,1:T(1,128)S(1)} %get-tuple-element.14) | copy-start | bytes 1540
  4.8 28.5 %all-to-all-start = ((s32[32,1,8]{2,1,0:T(1,128)}), s32[32,1,8]{2,1,0:T(1,128)S(1)}, u32[]{:S(2)}, u32[]{:S(2)}) async-start(s32[32,1,8]{2,1,0:T(1,128)} %bitcast.12), calls=%async_computation | async-start | bytes 32768 | tf_op jit(solution)/shard_map/all_to_all | solution.py:127
  28.4 32.6 %copy-start.2 = (f32[8,2048]{1,0:T(8,128)}, f32[8,2048]{1,0:T(8,128)S(1)}, u32[]{:S(2)}) copy-start(f32[8,2048]{1,0:T(8,128)S(1)} %get-tuple-element.30) | copy-start | bytes 196612
  28.4 32.6 %copy-start.4 = (f32[8,2048]{1,0:T(8,128)}, f32[8,2048]{1,0:T(8,128)S(1)}, u32[]{:S(2)}) copy-start(f32[8,2048]{1,0:T(8,128)S(1)} %get-tuple-element.31) | copy-start | bytes 196612
  33.3 27.6 %all-to-all-start.1 = ((f32[8,2,2,64]{0,2,1,3:T(2,128)}), f32[8,2,2,64]{0,2,1,3:T(2,128)S(1)}, u32[]{:S(2)}, u32[]{:S(2)}) async-start(f32[8,2,2,64]{0,2,1,3:T(2,128)} %copy.89), calls=%async_computation.1 | async-start | bytes 262144 | tf_op jit(solution)/shard_map/all_to_all | solution.py:108
  65.4 39.3 %all-to-all-start.2 = ((bf16[8,32,8,128]{3,0,2,1:T(8,128)(2,1)}), bf16[8,32,8,128]{3,0,2,1:T(8,128)(2,1)}, u32[]{:S(2)}, u32[]{:S(2)}) async-start(bf16[8,32,8,128]{3,0,2,1:T(8,128)(2,1)} %multiply_convert_fusion), calls=%async_computation.2 | async-start | bytes 1048576 | tf_op jit(solution)/shard_map/all_to_all | solution.py:135
  113.1 13.1 %copy-start.7 = (s32[16384]{0:T(1024)S(1)}, s32[16384]{0:T(1024)}, u32[]{:S(2)}) copy-start(s32[16384]{0:T(1024)} %get-tuple-element.23) | copy-start | bytes 196612
  126.2 115.6 %copy-start.6 = (f32[16384]{0:T(1024)S(1)}, f32[16384]{0:T(1024)}, u32[]{:S(2)}) copy-start(f32[16384]{0:T(1024)} %param.19) | copy-start | bytes 196612
  281.7 17.4 %all-to-all-start.3 = ((bf16[16,128,128]{2,1,0:T(8,128)(2,1)}), bf16[16,128,128]{2,1,0:T(8,128)(2,1)S(1)}, u32[]{:S(2)}, u32[]{:S(2)}) async-start(bf16[16,128,128]{2,1,0:T(8,128)(2,1)} %broadcast_in_dim.73), calls=%async_computation.3 | async-start | bytes 1048576 | tf_op jit(solution)/shard_map/all_to_all | solution.py:14
  424.1 91.3 %copy-start.10 = (s32[128,1]{0,1:T(1,128)S(1)}, s32[128,1]{0,1:T(1,128)}, u32[]{:S(2)}) copy-start(s32[128,1]{0,1:T(1,128)} %copy-done.9) | copy-start | bytes 1540
  509.4 21.3 %copy-start.8 = (s32[32,8]{1,0:T(8,128)S(1)}, s32[32,8]{1,0:T(8,128)}, u32[]{:S(2)}) copy-start(s32[32,8]{1,0:T(8,128)} %get-tuple-element.7) | copy-start | bytes 3076
  515.3 71.7 %copy-start.3 = (f32[8,2048]{1,0:T(8,128)S(1)}, f32[8,2048]{1,0:T(8,128)}, u32[]{:S(2)}) copy-start(f32[8,2048]{1,0:T(8,128)} %copy-done.2) | copy-start | bytes 196612
  515.3 71.7 %copy-start.5 = (f32[8,2048]{1,0:T(8,128)S(1)}, f32[8,2048]{1,0:T(8,128)}, u32[]{:S(2)}) copy-start(f32[8,2048]{1,0:T(8,128)} %copy-done.4) | copy-start | bytes 196612
  525.1 39.2 %all-to-all-start.4 = ((bf16[8,32,8,128]{3,2,0,1:T(8,128)(2,1)}), bf16[8,32,8,128]{3,2,0,1:T(8,128)(2,1)S(1)}, u32[]{:S(2)}, u32[]{:S(2)}) async-start(bf16[8,32,8,128]{3,2,0,1:T(8,128)(2,1)} %copy.97), calls=%async_computation.4 | async-start | bytes 1048576 | tf_op jit(solution)/shard_map/all_to_all | solution.py:163
where the time goes:
time: 599 us; the launch traced here: 597 us
  other arithmetic  278 us (46%)
  local copies, waits for them, and re-layouts  148 us (25%)
  waiting for transfers between devices  87.1 us (15%)
  starting transfers between devices  46.6 us (8%)
  blocking collectives  25.6 us (4%)
  matrix products  10.4 us (2%)
    scatter-add x1, other arithmetic, spread(): blank_grid = blank_grid.at[:, flat_low].add((1.0 - fractions) * weighted)  91.3 us
    scatter-add x1, other arithmetic, spread(): return blank_grid.at[:, flat_low + 1].add(fractions * weighted)  85.3 us
    gather x1, local copies, waits for them, and re-layouts, interpolate(): flat_values[:, flat_low + 1]  57.8 us
    gather x1, local copies, waits for them, and re-layouts, interpolate(): flat_values[:, flat_low]  57.8 us
    reduce_sum x1, other arithmetic, local(): partial_value = jnp.sum(own_turn * values, axis=0)  39 us
    all_to_all x1, waiting for transfers between devices, local(): lax.all_to_all(back_slots.reshape(local_orders, ma_count, capacity, block...  33.4 us
    mul x1, other arithmetic, spread(): return blank_grid.at[:, flat_low + 1].add(fractions * weighted)  33.4 us
    all_to_all x1, waiting for transfers between devices, local(): lax.all_to_all(outgoing.reshape(local_orders, ma_count, capacity, block_c...  30.6 us
  transfers between devices with their start and end apart: 5, of which 5 were waited for; matrix products, arithmetic and copies ran while one was open for 3% of the time, Pallas kernels for 0%

commit v1 on v0

v1 whole, which is shorter than its diff:
```python
import functools
import math

import jax
import jax.numpy as jnp
from jax import lax
from jax.experimental import pallas as pl
from jax.experimental.pallas import tpu as pltpu
from jax.sharding import PartitionSpec as P

F32 = jnp.float32
BF16 = jnp.bfloat16
I32 = jnp.int32

COS_TURNS = (
    0.99999997389483,
    -19.739202931827737,
    64.93907559492132,
    -85.44969773655134,
    60.1656143595228,
    -25.96416606164654,
    6.528151014475474,
)
N_MA = 32
N_BEAM = 16
KL = 8
PHI_BLOCKS = 32
NSB = 128


def cos_turns(turns):
    v = turns - jnp.floor(turns + 0.5)
    w = v * v
    acc = jnp.full_like(w, COS_TURNS[-1])
    for coef in COS_TURNS[-2::-1]:
        acc = acc * w + coef
    return acc


def nn(a, b):
    return lax.dot_general(a, b, (((1,), (0,)), ((), ())), preferred_element_type=F32)


def nt(a, b):
    return lax.dot_general(a, b, (((1,), (1,)), ((), ())), preferred_element_type=F32)


def split(x):
    high = x.astype(BF16)
    return high, (x - high.astype(F32)).astype(BF16)


def kernel(
    owner_s,
    local_s,
    order_s,
    count_s,
    owner_ref,
    local_ref,
    sky_hbm,
    beam_hbm,
    wig_hbm,
    offset_hbm,
    fraction_hbm,
    angle_hbm,
    noise_hbm,
    out_ref,
    sky,
    beam,
    wig,
    offset,
    fraction,
    angle,
    noise,
    order,
    phase,
    turn,
    interp,
    rows,
    piece,
    gathered,
    gathered_f,
    modes,
    partial,
    signals,
    filtered,
    gmat,
    gout_f,
    gout,
    gin,
    fin,
    fin_in,
    load_sem,
    wig_sem,
    ag_send,
    ag_recv,
    rs_send,
    rs_recv,
    fl_send,
    fl_recv,
    gr_send,
    gr_recv,
    fin_send,
    fin_recv,
):
    me_a = lax.axis_index("ma")
    me_b = lax.axis_index("beam")

    loads = [
        pltpu.make_async_copy(src, dst, load_sem.at[i])
        for i, (src, dst) in enumerate(
            [
                (beam_hbm, beam),
                (sky_hbm, sky),
                (offset_hbm, offset),
                (fraction_hbm, fraction),
                (angle_hbm, angle),
                (noise_hbm, noise),
            ]
        )
    ]
    wig_loads = [
        pltpu.make_async_copy(wig_hbm.at[pl.ds(2 * i, 2)], wig.at[pl.ds(2 * i, 2)], wig_sem.at[i])
        for i in range(4)
    ]
    loads[0].start()
    loads[1].start()
    for copy in wig_loads:
        copy.start()
    for copy in loads[2:]:
        copy.start()

    barrier = pltpu.get_barrier_semaphore()

    def greet_ma(i, _):
        pl.semaphore_signal(barrier, inc=1, device_id={"ma": lax.rem(me_a + i, N_MA)})
        return 0

    def greet_beam(i, _):
        pl.semaphore_signal(barrier, inc=1, device_id={"beam": lax.rem(me_b + i, N_BEAM)})
        return 0

    lax.fori_loop(1, N_MA, greet_ma, 0)
    lax.fori_loop(1, N_BEAM, greet_beam, 0)

    def far_first(i):
        half = (i + 1) // 2
        return lax.rem(me_a + N_MA + 16 + half * (1 - 2 * lax.rem(i, 2)), N_MA)

    def copy_ma(src, dst, send, recv, peer):
        return pltpu.make_async_remote_copy(
            src_ref=src,
            dst_ref=dst,
            send_sem=send.at[peer],
            recv_sem=recv.at[me_a],
            device_id={"ma": peer},
        )

    def copy_beam(src, dst, send, recv, peer):
        return pltpu.make_async_remote_copy(
            src_ref=src,
            dst_ref=dst,
            send_sem=send.at[peer],
            recv_sem=recv.at[me_b],
            device_id={"beam": peer},
        )

    def came(dst, send, recv, source):
        return pltpu.make_async_remote_copy(
            src_ref=dst,
            dst_ref=dst,
            send_sem=send.at[source],
            recv_sem=recv.at[source],
            device_id={"ma": me_a},
        )

    loads[0].wait()
    loads[1].wait()
    beam_re = beam[:, 0, :]
    beam_im = beam[:, 1, :]
    products = []
    for m in range(2):
        sky_re = sky[m, 0:1, :]
        sky_im = sky[m, 1:2, :]
        products.append(
            jnp.concatenate(
                [sky_re * beam_re - sky_im * beam_im, sky_re * beam_im + sky_im * beam_re], axis=0
            ).astype(BF16)
        )
    sub = lax.broadcasted_iota(I32, (KL, 128), 0)
    lane = lax.broadcasted_iota(I32, (KL, 128), 1)
    for quad in range(2):
        wig_loads[2 * quad].wait()
        wig_loads[2 * quad + 1].wait()
        for m in range(2):
            weights = jnp.concatenate([wig[4 * quad + k, m] for k in range(4)], axis=0)
            out = nt(products[m], weights)
            for pair in range(2):
                kp = 2 * quad + pair
                keep = sub == 2 * kp + lane // 64
                for c in range(2):
                    part = out[c * KL : (c + 1) * KL, pair * 128 : (pair + 1) * 128]
                    row = (m * 2 + c) * 4 + kp
                    rows[row : row + 1, :] = jnp.sum(
                        jnp.where(keep, part, 0.0), axis=0, keepdims=True
                    )
    piece[...] = rows[...].astype(BF16)

    pl.semaphore_wait(barrier, N_MA - 1 + N_BEAM - 1)

    def send_modes(i, _):
        copy_ma(piece, gathered.at[me_a], ag_send, ag_recv, far_first(i)).start()
        return 0

    lax.fori_loop(0, N_MA - 1, send_modes, 0)
    gathered[me_a] = piece[...]

    for copy in loads[2:]:
        copy.wait()
    for m in range(64):
        order[2 * m : 2 * m + 2, :] = jnp.full((2, 128), order_s[m], I32)
    quarter = (lax.broadcasted_iota(I32, (128, 128), 0) % 2).astype(F32) * 0.25

    def phases(b, _):
        cells = (b * 128 + lax.broadcasted_iota(I32, (128, 128), 1)).astype(F32) * (1.0 / 4096.0)
        turns = order[...].astype(F32) * cells + quarter
        high, low = split(cos_turns(turns) * 0.125)
        phase[b] = jnp.concatenate([high, low], axis=1)
        return 0

    lax.fori_loop(0, PHI_BLOCKS, phases, 0)

    beam_order = me_b * KL + sub
    spin = ((beam_order + 1) // 2).astype(F32)
    back = (beam_order % 2).astype(F32) * 0.25

    def turns_of(s, _):
        around = angle[pl.ds(s, 1), :] * (1.0 / (2.0 * math.pi))
        turn[s] = cos_turns(spin * around - back) * (1.0 / math.sqrt(128.0))
        return 0

    lax.fori_loop(0, NSB, turns_of, 0, unroll=4)

    cell = lax.broadcasted_iota(I32, (128, 128), 0)

    def interpolators(s, _):
        block = lax.rem(local_s[s], PHI_BLOCKS)
        low = offset[pl.ds(s, 1), :]
        right = fraction[pl.ds(s, 1), :]
        mix = jnp.where(
            cell == low, 1.0 - right, jnp.where(cell == low + 1, right, 0.0)
        ).astype(BF16)
        interp[s] = nn(phase[block], jnp.concatenate([mix, mix], axis=0)).astype(BF16)
        return 0

    lax.fori_loop(0, NSB, interpolators, 0, unroll=4)

    def modes_arrive(i, _):
        source = far_first(N_MA - 2 - i)
        came(gathered.at[source], ag_send, ag_recv, source).wait_recv()
        return 0

    lax.fori_loop(0, N_MA - 1, modes_arrive, 0)
    gathered_f[...] = gathered[...].astype(F32).reshape(512, 128)
    for kp in range(4):
        block = gathered_f[pl.ds(kp, 128, stride=4), :].T
        modes[:, 2 * kp, :] = block[:64]
        modes[:, 2 * kp + 1, :] = block[64:]

    def octet(i, _):
        peer = lax.rem(me_b + 1 + i, N_BEAM)
        for j in range(8):
            s = peer * 8 + j
            cycle = owner_s[s] * 2 + lax.div(local_s[s], PHI_BLOCKS)
            own = modes[cycle].astype(BF16)
            values = nn(own, interp[s])
            partial[peer, j : j + 1, :] = jnp.sum(turn[s] * values, axis=0, keepdims=True)

        @pl.when(i < N_BEAM - 1)
        def _():
            copy_beam(partial.at[peer], signals.at[me_b], rs_send, rs_recv, peer).start()

        return 0

    lax.fori_loop(0, N_BEAM, octet, 0)

    def signals_arrive(i, total):
        source = lax.rem(me_b + N_BEAM - 1 - i, N_BEAM)
        came(signals.at[source], rs_send, rs_recv, source).wait_recv()
        return total + signals[source]

    total = lax.fori_loop(0, N_BEAM - 1, signals_arrive, partial[me_b])
    stamps = (
        (me_b * 8 + lax.broadcasted_iota(I32, (8, 128), 0)) * 128
        + lax.broadcasted_iota(I32, (8, 128), 1)
    )
    valid = (stamps < count_s[0]).astype(F32)
    filtered[me_b] = (
        lax.dot_general(
            total * valid,
            noise[...],
            (((1,), (1,)), ((), ())),
            precision=lax.Precision.HIGHEST,
            preferred_element_type=F32,
        )
        * valid
    )

    def send_filtered(i, _):
        peer = lax.rem(me_b + 1 + i, N_BEAM)
        copy_beam(filtered.at[me_b], filtered.at[me_b], fl_send, fl_recv, peer).start()
        return 0

    lax.fori_loop(0, N_BEAM - 1, send_filtered, 0)

    def adjoint(i, _):
        source = lax.rem(me_b + N_BEAM - i, N_BEAM)

        @pl.when(i > 0)
        def _():
            came(filtered.at[source], fl_send, fl_recv, source).wait_recv()

        eight = filtered[source]
        for j in range(8):
            s = source * 8 + j
            high, low = split(turn[s] * eight[j : j + 1, :])
            both = nt(jnp.concatenate([high, low], axis=0), interp[s])
            gmat[pl.ds(pl.multiple_of(s * KL, KL), KL), :] = both[:KL] + both[KL:]
        return 0

    lax.fori_loop(0, N_BEAM, adjoint, 0)

    cycles = owner_ref[...] * 2 + lax.div(local_ref[...], jnp.full((1, NSB), PHI_BLOCKS, I32))
    pick = (lax.broadcasted_iota(I32, (64, 128), 0) == cycles).astype(F32).astype(BF16)
    pick = jnp.concatenate([pick, pick], axis=1)
    for kp in range(4):
        halves = []
        for k in (2 * kp, 2 * kp + 1):
            high, low = split(gmat[pl.ds(k, 128, stride=KL), :])
            halves.append(nn(pick, jnp.concatenate([high, low], axis=0)))
        gout_f[pl.ds(kp, 128, stride=4), :] = jnp.concatenate(halves, axis=0).T
    gout[...] = gout_f[...].reshape(N_MA, 16, 128).astype(BF16)

    def send_grads(i, _):
        peer = far_first(i)
        copy_ma(gout.at[peer], gin.at[me_a], gr_send, gr_recv, peer).start()
        return 0

    lax.fori_loop(0, N_MA - 1, send_grads, 0)

    def grads_arrive(i, acc):
        source = far_first(N_MA - 2 - i)
        came(gin.at[source], gr_send, gr_recv, source).wait_recv()
        return acc + gin[source].astype(F32)

    rows[...] = lax.fori_loop(0, N_MA - 1, grads_arrive, gout[me_a].astype(F32))

    for m in range(2):
        lhs = []
        for c in range(2):
            for kp in range(4):
                row = (m * 2 + c) * 4 + kp
                spreadout = jnp.broadcast_to(rows[row : row + 1, :], (KL, 128))
                lhs.append(jnp.where(sub == 2 * kp + lane // 64, spreadout, 0.0))
        lhs = jnp.concatenate(
            [jnp.concatenate(lhs[:4], axis=1), jnp.concatenate(lhs[4:], axis=1)], axis=0
        ).astype(BF16)
        weights = jnp.concatenate([wig[k, m] for k in range(KL)], axis=0)
        harm = nn(lhs, weights)
        re, im = harm[:KL], harm[KL:]
        first = jnp.sum(re * beam_re + im * beam_im, axis=0, keepdims=True)
        second = jnp.sum(im * beam_re - re * beam_im, axis=0, keepdims=True)
        for b in range(N_BEAM):
            fin[b, 2 * m : 2 * m + 1, :] = first[:, b * 128 : (b + 1) * 128]
            fin[b, 2 * m + 1 : 2 * m + 2, :] = second[:, b * 128 : (b + 1) * 128]

    def send_final(i, _):
        peer = lax.rem(me_b + 1 + i, N_BEAM)
        copy_beam(fin.at[peer], fin_in.at[me_b], fin_send, fin_recv, peer).start()
        return 0

    lax.fori_loop(0, N_BEAM - 1, send_final, 0)

    def final_arrive(i, acc):
        source = lax.rem(me_b + N_BEAM - 1 - i, N_BEAM)
        came(fin_in.at[source], fin_send, fin_recv, source).wait_recv()
        return acc + fin_in[source]

    result = lax.fori_loop(0, N_BEAM - 1, final_arrive, fin[me_b])
    out_ref[0] = result[0:2]
    out_ref[1] = result[2:4]

    def sent_ma(i, _):
        peer = lax.rem(me_a + 1 + i, N_MA)
        copy_ma(piece, gathered.at[me_a], ag_send, ag_recv, peer).wait_send()
        copy_ma(gout.at[peer], gin.at[me_a], gr_send, gr_recv, peer).wait_send()
        return 0

    lax.fori_loop(0, N_MA - 1, sent_ma, 0)

    def sent_beam(i, _):
        peer = lax.rem(me_b + 1 + i, N_BEAM)
        copy_beam(partial.at[peer], signals.at[me_b], rs_send, rs_recv, peer).wait_send()
        copy_beam(filtered.at[me_b], filtered.at[me_b], fl_send, fl_recv, peer).wait_send()
        copy_beam(fin.at[peer], fin_in.at[me_b], fin_send, fin_recv, peer).wait_send()
        return 0

    lax.fori_loop(0, N_BEAM - 1, sent_beam, 0)


def local(
    sky_harmonics,
    beam_harmonics,
    wigner,
    order_map,
    block_owner,
    block_local,
    cell_offset,
    cell_fraction,
    beam_angle,
    sample_count,
    noise_weight,
):
    smem = pl.BlockSpec(memory_space=pltpu.SMEM)
    vmem = pl.BlockSpec(memory_space=pltpu.VMEM)
    hbm = pl.BlockSpec(memory_space=pl.ANY)
    dma = pltpu.SemaphoreType.DMA
    owner = block_owner.reshape(NSB)
    return pl.pallas_call(
        kernel,
        out_shape=jax.ShapeDtypeStruct((2, 2, 128), F32),
        in_specs=[smem] * 4 + [vmem] * 2 + [hbm] * 7,
        out_specs=vmem,
        scratch_shapes=[
            pltpu.VMEM((2, 2, 2048), F32),
            pltpu.VMEM((KL, 2, 2048), F32),
            pltpu.VMEM((KL, 2, 64, 2048), BF16),
            pltpu.VMEM((NSB, 128), I32),
            pltpu.VMEM((NSB, 128), F32),
            pltpu.VMEM((NSB, 128), F32),
            pltpu.VMEM((128, 128), F32),
            pltpu.VMEM((128, 128), I32),
            pltpu.VMEM((PHI_BLOCKS, 128, 256), BF16),
            pltpu.VMEM((NSB, KL, 128), F32),
            pltpu.VMEM((NSB, 128, 128), BF16),
            pltpu.VMEM((16, 128), F32),
            pltpu.VMEM((16, 128), BF16),
            pltpu.VMEM((N_MA, 16, 128), BF16),
            pltpu.VMEM((512, 128), F32),
            pltpu.VMEM((64, KL, 128), F32),
            pltpu.VMEM((N_BEAM, 8, 128), F32),
            pltpu.VMEM((N_BEAM, 8, 128), F32),
            pltpu.VMEM((N_BEAM, 8, 128), F32),
            pltpu.VMEM((NSB * KL, 128), F32),
            pltpu.VMEM((512, 128), F32),
            pltpu.VMEM((N_MA, 16, 128), BF16),
            pltpu.VMEM((N_MA, 16, 128), BF16),
            pltpu.VMEM((N_BEAM, 4, 128), F32),
            pltpu.VMEM((N_BEAM, 4, 128), F32),
            dma((6,)),
            dma((4,)),
            dma((N_MA,)),
            dma((N_MA,)),
            dma((N_BEAM,)),
            dma((N_BEAM,)),
            dma((N_BEAM,)),
            dma((N_BEAM,)),
            dma((N_MA,)),
            dma((N_MA,)),
            dma((N_BEAM,)),
            dma((N_BEAM,)),
        ],
        compiler_params=pltpu.CompilerParams(collective_id=0, has_side_effects=True),
        name="normal_operator",
    )(
        owner,
        block_local,
        order_map,
        sample_count,
        owner.reshape(1, NSB),
        block_local.reshape(1, NSB),
        sky_harmonics,
        beam_harmonics,
        wigner,
        cell_offset.reshape(NSB, 128),
        cell_fraction.reshape(NSB, 128),
        beam_angle.reshape(NSB, 128),
        noise_weight,
    )


def solution(mesh):
    return jax.shard_map(
        local,
        mesh=mesh,
        in_specs=(
            P("ma", None, None),
            P("beam", None, None),
            P("beam", "ma", None, None),
            P(),
            P("ma", None),
            P("ma"),
            P("ma"),
            P("ma"),
            P("ma"),
            P("ma"),
            P(),
        ),
        out_specs=P("ma", None, "beam"),
        check_vma=False,
    )
```

time: 599 us -> 60.8 us (0.10)
  other arithmetic: 278 us -> 0 us
  local copies, waits for them, and re-layouts: 148 us -> 1.26 us
  waiting for transfers between devices: 87.1 us -> 0 us
  Pallas kernels: 0 us -> 58.7 us
  starting transfers between devices: 46.6 us -> 0 us
  blocking collectives: 25.6 us -> 0 us
  matrix products: 10.4 us -> 0 us
    scatter-add x2 -> x0, other arithmetic: 177 us -> none  [the longest x1 91.3 us: spread(): blank_grid = blank_grid.at[:, flat_low].add((1.0 - fractions) * weighted)]
    gather x5 -> x0, local copies, waits for them, and re-layouts: 124 us -> none  [the longest x1 57.8 us: interpolate(): flat_values[:, flat_low + 1]]
    all_to_all x5 -> x0, waiting for transfers between devices: 87.1 us -> none  [the longest x1 33.4 us: local(): lax.all_to_all(back_slots.reshape(local_orders, ma_count, capacity, block...]
    pallas_call x0 -> x1, Pallas kernels: none -> 58.7 us  [local(): pl.pallas_call(kernel, out_shape=jax.ShapeDtypeStruct((2, 2, 128), F32),...]
    all_to_all x5 -> x0, starting transfers between devices: 46.6 us -> none  [the longest x1 16.7 us: local(): lax.all_to_all(requests, 'ma', split_axis=0, concat_axis=0, tiled=True)]
    reduce_sum x5 -> x0, other arithmetic: 40.1 us -> none  [the longest x1 39 us: local(): partial_value = jnp.sum(own_turn * values, axis=0)]
    mul x2 -> x0, other arithmetic: 33.4 us -> none  [the longest x1 33.4 us: spread(): return blank_grid.at[:, flat_low + 1].add(fractions * weighted)]
    all_to_all x2 -> x0, blocking collectives: 25.6 us -> none  [the longest x1 16.4 us: local(): lax.all_to_all(grad_modes, 'ma', split_axis=1, concat_axis=3, tiled=True)]
  transfers between devices with their start and end apart: 5 -> 0, of which waited for: 5 -> 0; matrix products, arithmetic and copies ran while one was open for 3% -> 0% of each run, Pallas kernels for 0% -> 0%
where the time goes in v1:
time: 60.8 us; the launch traced here: 60.6 us
  Pallas kernels  58.7 us (97%)
  local copies, waits for them, and re-layouts  1.26 us (2%)
  between operations  0.66 us (1%)
    pallas_call x1, Pallas kernels, local(): pl.pallas_call(kernel, out_shape=jax.ShapeDtypeStruct((2, 2, 128), F32),...  58.7 us
    unnamed x1, local copies, waits for them, and re-layouts  1.26 us

profile of v1, /device:TPU:1, one launch (start us, length us, event | category | flops | bytes accessed | tf_op | source)
XLA Modules:
  0.0 60.6 jit_solution(11175073029254122043)
XLA Ops:
  0.7 58.7 %normal_operator.1 = f32[2,2,128]{2,1,0:T(2,128)} custom-call(s32[128]{0:T(128)} %bitcast.9, s32[128]{0:T(128)} %local_s.1, s32[64]{0:T(128)} %order_s.1, s32[1]{0:T(128)S(6)} %copy.13.count_s, s32[1,128]{1,0:T(1,128)} %bitcast.10, s32[1,128]{1,0:T(1,128)} %bitcast.11, f32[2,2,2048]{2,1,0:T(2,128)} %sky_hbm.1, f32[8,2,2048]{2,1,0:T(2,128)} %beam_hbm.1, ...), custom_call_target="tpu_custom_call" | custom-call | tf_op jit(solution)/shard_map/normal_operator/pallas_call | solution.py:429
  59.3 1.3 %copy.14 = f32[2,2,128]{2,1,0:T(2,128)} copy(f32[2,2,128]{2,1,0:T(2,128)} %normal_operator.1) | data formatting | bytes 4096

commit v2 on v1

v2 whole, which is shorter than its diff:
```python
import functools
import math

import jax
import jax.numpy as jnp
from jax import lax
from jax.experimental import pallas as pl
from jax.experimental.pallas import tpu as pltpu
from jax.sharding import PartitionSpec as P

F32 = jnp.float32
BF16 = jnp.bfloat16
I32 = jnp.int32

COS_TURNS = (
    0.99999997389483,
    -19.739202931827737,
    64.93907559492132,
    -85.44969773655134,
    60.1656143595228,
    -25.96416606164654,
    6.528151014475474,
)
N_MA = 32
N_BEAM = 16
KL = 8
PHI_BLOCKS = 32
NSB = 128


def cos_turns(turns):
    v = turns - jnp.floor(turns + 0.5)
    w = v * v
    acc = jnp.full_like(w, COS_TURNS[-1])
    for coef in COS_TURNS[-2::-1]:
        acc = acc * w + coef
    return acc


def nn(a, b):
    return lax.dot_general(a, b, (((1,), (0,)), ((), ())), preferred_element_type=F32)


def nt(a, b):
    return lax.dot_general(a, b, (((1,), (1,)), ((), ())), preferred_element_type=F32)


def split(x):
    high = x.astype(BF16)
    return high, (x - high.astype(F32)).astype(BF16)


def kernel(
    owner_hbm,
    local_hbm,
    order_hbm,
    count_s,
    owner_row_hbm,
    local_row_hbm,
    sky_hbm,
    beam_hbm,
    wig_hbm,
    offset_hbm,
    fraction_hbm,
    angle_hbm,
    noise_hbm,
    out_ref,
    owner_s,
    local_s,
    order_s,
    owner_row,
    local_row,
    sky,
    beam,
    wig,
    offset,
    fraction,
    angle,
    noise,
    order,
    phase,
    turn,
    interp,
    rows,
    piece,
    gathered,
    gathered_f,
    modes,
    partial,
    sum_out,
    sum_in,
    sum2_out,
    sum2_in,
    filtered,
    gmat,
    gout_f,
    gpair,
    gout,
    gin,
    fin,
    fin_in,
    load_sem,
    wig_sem,
    ag_send,
    ag_recv,
    agp_send,
    agp_recv,
    s1_send,
    s1_recv,
    s2_send,
    s2_recv,
    grp_send,
    grp_recv,
    gr_send,
    gr_recv,
    fin_send,
    fin_recv,
):
    me_a = lax.axis_index("ma")
    me_b = lax.axis_index("beam")
    z = lax.div(me_a, 2)
    core = lax.rem(me_a, 2)
    x = lax.rem(me_b, 4)
    y = lax.div(me_b, 4)

    loads = [
        pltpu.make_async_copy(src, dst, load_sem.at[i])
        for i, (src, dst) in enumerate(
            [
                (beam_hbm, beam),
                (sky_hbm, sky),
                (order_hbm, order_s),
                (angle_hbm, angle),
                (local_hbm, local_s),
                (owner_hbm, owner_s),
                (offset_hbm, offset),
                (fraction_hbm, fraction),
                (owner_row_hbm, owner_row),
                (local_row_hbm, local_row),
                (noise_hbm, noise),
            ]
        )
    ]
    wig_loads = [
        pltpu.make_async_copy(wig_hbm.at[pl.ds(2 * i, 2)], wig.at[pl.ds(2 * i, 2)], wig_sem.at[i])
        for i in range(4)
    ]
    loads[0].start()
    loads[1].start()
    for copy in wig_loads:
        copy.start()

    barrier = pltpu.get_barrier_semaphore()

    def far_z(i):
        half = (i + 1) // 2
        return lax.rem(z + 16 + 8 + half * (1 - 2 * lax.rem(i, 2)), 16)

    def greet_z(i, _):
        pl.semaphore_signal(barrier, inc=1, device_id={"ma": far_z(i) * 2 + core})
        return 0

    def greet_beam(i, _):
        pl.semaphore_signal(barrier, inc=1, device_id={"beam": lax.rem(me_b + i, N_BEAM)})
        return 0

    partner = z * 2 + 1 - core
    lax.fori_loop(0, 15, greet_z, 0)
    lax.fori_loop(1, N_BEAM, greet_beam, 0)
    pl.semaphore_signal(barrier, inc=1, device_id={"ma": partner})
    for copy in loads[2:]:
        copy.start()

    def remote(src, dst, send, recv, **peer):
        return pltpu.make_async_remote_copy(
            src_ref=src, dst_ref=dst, send_sem=send, recv_sem=recv, device_id=peer
        )

    def to_z(src, dst, send, recv, peer):
        return remote(src, dst, send.at[peer], recv.at[z], ma=peer * 2 + core)

    def to_beam(src, dst, send, recv, peer):
        return remote(src, dst, send.at[peer], recv.at[me_b], beam=peer)

    def came(dst, send, recv):
        return remote(dst, dst, send, recv, ma=me_a)

    loads[0].wait()
    loads[1].wait()
    beam_re = beam[:, 0, :]
    beam_im = beam[:, 1, :]
    products = []
    for m in range(2):
        sky_re = sky[m, 0:1, :]
        sky_im = sky[m, 1:2, :]
        products.append(
            jnp.concatenate(
                [sky_re * beam_re - sky_im * beam_im, sky_re * beam_im + sky_im * beam_re], axis=0
            ).astype(BF16)
        )
    sub = lax.broadcasted_iota(I32, (KL, 128), 0)
    lane = lax.broadcasted_iota(I32, (KL, 128), 1)
    for quad in range(2):
        wig_loads[2 * quad].wait()
        wig_loads[2 * quad + 1].wait()
        for m in range(2):
            weights = jnp.concatenate([wig[4 * quad + k, m] for k in range(4)], axis=0)
            out = nt(products[m], weights)
            for pair in range(2):
                kp = 2 * quad + pair
                keep = sub == 2 * kp + lane // 64
                for c in range(2):
                    part = out[c * KL : (c + 1) * KL, pair * 128 : (pair + 1) * 128]
                    row = (m * 2 + c) * 4 + kp
                    rows[row : row + 1, :] = jnp.sum(
                        jnp.where(keep, part, 0.0), axis=0, keepdims=True
                    )
    piece[...] = rows[...].astype(BF16)

    pl.semaphore_wait(barrier, 15 + 15 + 1)

    def send_modes(i, _):
        to_z(piece, gathered.at[core, z], ag_send, ag_recv, far_z(i)).start()
        return 0

    lax.fori_loop(0, 15, send_modes, 0)
    gathered[core, z] = piece[...]

    for copy in loads[2:]:
        copy.wait()
    for a_core in range(2):
        for a_z in range(16):
            for m in range(2):
                row = (a_core * 16 + a_z) * 4 + m * 2
                order[row : row + 2, :] = jnp.full((2, 128), order_s[(a_z * 2 + a_core) * 2 + m], I32)
    quarter = (lax.broadcasted_iota(I32, (128, 128), 0) % 2).astype(F32) * 0.25

    def phases(b, _):
        cells = (b * 128 + lax.broadcasted_iota(I32, (128, 128), 1)).astype(F32) * (1.0 / 4096.0)
        turns = order[...].astype(F32) * cells + quarter
        high, low = split(cos_turns(turns) * 0.125)
        phase[b] = jnp.concatenate([high, low], axis=1)
        return 0

    lax.fori_loop(0, PHI_BLOCKS, phases, 0)

    beam_order = me_b * KL + sub
    spin = ((beam_order + 1) // 2).astype(F32)
    back = (beam_order % 2).astype(F32) * 0.25

    def turns_of(s, _):
        around = angle[pl.ds(s, 1), :] * (1.0 / (2.0 * math.pi))
        turn[s] = cos_turns(spin * around - back) * (1.0 / math.sqrt(128.0))
        return 0

    lax.fori_loop(0, NSB, turns_of, 0, unroll=4)

    cell = lax.broadcasted_iota(I32, (128, 128), 0)

    def interpolators(s, _):
        block = lax.rem(local_s[s], PHI_BLOCKS)
        low = offset[pl.ds(s, 1), :]
        right = fraction[pl.ds(s, 1), :]
        mix = jnp.where(
            cell == low, 1.0 - right, jnp.where(cell == low + 1, right, 0.0)
        ).astype(BF16)
        interp[s] = nn(phase[block], jnp.concatenate([mix, mix], axis=0)).astype(BF16)
        return 0

    lax.fori_loop(0, NSB, interpolators, 0, unroll=4)

    def modes_arrive(i, _):
        source = far_z(14 - i)
        came(gathered.at[core, source], ag_send.at[source], ag_recv.at[source]).wait_recv()
        return 0

    lax.fori_loop(0, 15, modes_arrive, 0)
    swap_modes = remote(gathered.at[core], gathered.at[core], agp_send, agp_recv, ma=partner)
    swap_modes.start()
    came(gathered.at[1 - core], agp_send, agp_recv).wait_recv()
    gathered_f[...] = gathered[...].astype(F32).reshape(512, 128)
    for kp in range(4):
        block = gathered_f[pl.ds(kp, 128, stride=4), :].T
        modes[:, 2 * kp, :] = block[:64]
        modes[:, 2 * kp + 1, :] = block[64:]

    def forward(first, rows_at):
        for j in range(16):
            s = first + j
            cycle = owner_s[s] * 2 + lax.div(local_s[s], PHI_BLOCKS)
            values = nn(modes[cycle].astype(BF16), interp[s])
            partial[rows_at + j : rows_at + j + 1, :] = jnp.sum(
                turn[s] * values, axis=0, keepdims=True
            )

    def along_x(i):
        return y * 4 + lax.rem(x + i, 4)

    def along_y(i):
        return lax.rem(y + i, 4) * 4 + x

    def exchange(chunk, stage, out, into, send, recv):
        x_first = chunk < 2
        use_x = x_first if stage == 0 else not x_first
        mine = x if use_x else y
        copies = []
        for i in range(1, 4):
            peer = along_x(i) if use_x else along_y(i)
            copies.append(
                remote(
                    out.at[chunk],
                    into.at[chunk, mine],
                    send.at[chunk, i],
                    recv.at[chunk, mine],
                    beam=peer,
                )
            )
        return copies

    def collect(chunk, stage, own, into, send, recv):
        x_first = chunk < 2
        use_x = x_first if stage == 0 else not x_first
        mine = x if use_x else y
        total = own
        for i in range(1, 4):
            source = lax.rem(mine + i, 4)
            came(into.at[chunk, source], send.at[chunk, i], recv.at[chunk, source]).wait_recv()
            total = total + into[chunk, source].astype(F32)
        return total

    first_stage = [exchange(c, 0, sum_out, sum_in, s1_send, s1_recv) for c in range(4)]
    second_stage = [exchange(c, 1, sum2_out, sum2_in, s2_send, s2_recv) for c in range(4)]
    sequence = (0, 2, 1, 3)
    for chunk in sequence:
        forward(chunk * 32, 0)
        forward(chunk * 32 + 16, 16)
        sum_out[chunk] = partial[...].astype(BF16)
        for copy in first_stage[chunk]:
            copy.start()
    for chunk in sequence:
        total = collect(chunk, 0, sum_out[chunk].astype(F32), sum_in, s1_send, s1_recv)
        sum2_out[chunk] = total.astype(BF16)
        for copy in second_stage[chunk]:
            copy.start()

    def backward(first, rows_at):
        for j in range(16):
            s = first + j
            high, low = split(turn[s] * filtered[rows_at + j : rows_at + j + 1, :])
            both = nt(jnp.concatenate([high, low], axis=0), interp[s])
            gmat[s * KL : (s + 1) * KL, :] = both[:KL] + both[KL:]

    for chunk in sequence:
        signal = collect(chunk, 1, sum2_out[chunk].astype(F32), sum2_in, s2_send, s2_recv)
        stamps = (
            chunk * 32 + lax.broadcasted_iota(I32, (32, 128), 0)
        ) * 128 + lax.broadcasted_iota(I32, (32, 128), 1)
        valid = (stamps < count_s[0]).astype(F32)
        filtered[...] = (
            lax.dot_general(
                signal * valid,
                noise[...],
                (((1,), (1,)), ((), ())),
                precision=lax.Precision.HIGHEST,
                preferred_element_type=F32,
            )
            * valid
        )
        backward(chunk * 32, 0)
        backward(chunk * 32 + 16, 16)

    cycles = owner_row[...] * 2 + lax.div(local_row[...], jnp.full((1, NSB), PHI_BLOCKS, I32))
    pick = (lax.broadcasted_iota(I32, (64, 128), 0) == cycles).astype(F32).astype(BF16)
    pick = jnp.concatenate([pick, pick], axis=1)
    for kp in range(4):
        halves = []
        for k in (2 * kp, 2 * kp + 1):
            high, low = split(gmat[pl.ds(k, 128, stride=KL), :])
            halves.append(nn(pick, jnp.concatenate([high, low], axis=0)))
        gout_f[pl.ds(kp, 128, stride=4), :] = jnp.concatenate(halves, axis=0).T

    half_rows = pl.multiple_of(core * 256, 256)
    other_rows = pl.multiple_of((1 - core) * 256, 256)
    swap_grads = remote(gout_f.at[pl.ds(other_rows, 256)], gpair, grp_send, grp_recv, ma=partner)
    swap_grads.start()
    swap_modes.wait_send()

    def sent_modes(i, _):
        peer = far_z(i)
        to_z(piece, gathered.at[core, z], ag_send, ag_recv, peer).wait_send()
        return 0

    lax.fori_loop(0, 15, sent_modes, 0)
    came(gpair, grp_send, grp_recv).wait_recv()
    gout[...] = (gout_f[pl.ds(half_rows, 256), :] + gpair[...]).reshape(16, 16, 128).astype(BF16)

    def send_grads(i, _):
        peer = far_z(i)
        to_z(gout.at[peer], gin.at[z], gr_send, gr_recv, peer).start()
        return 0

    lax.fori_loop(0, 15, send_grads, 0)
    for chunk in range(4):
        for copy in first_stage[chunk] + second_stage[chunk]:
            copy.wait_send()
    swap_grads.wait_send()

    def grads_arrive(i, acc):
        source = far_z(14 - i)
        came(gin.at[source], gr_send.at[source], gr_recv.at[source]).wait_recv()
        return acc + gin[source].astype(F32)

    rows[...] = lax.fori_loop(0, 15, grads_arrive, gout[z].astype(F32))

    for m in range(2):
        lhs = []
        for c in range(2):
            for kp in range(4):
                row = (m * 2 + c) * 4 + kp
                spreadout = jnp.broadcast_to(rows[row : row + 1, :], (KL, 128))
                lhs.append(jnp.where(sub == 2 * kp + lane // 64, spreadout, 0.0))
        lhs = jnp.concatenate(
            [jnp.concatenate(lhs[:4], axis=1), jnp.concatenate(lhs[4:], axis=1)], axis=0
        ).astype(BF16)
        weights = jnp.concatenate([wig[k, m] for k in range(KL)], axis=0)
        harm = nn(lhs, weights)
        re, im = harm[:KL], harm[KL:]
        first = jnp.sum(re * beam_re + im * beam_im, axis=0, keepdims=True)
        second = jnp.sum(im * beam_re - re * beam_im, axis=0, keepdims=True)
        for b in range(N_BEAM):
            fin[b, 2 * m : 2 * m + 1, :] = first[:, b * 128 : (b + 1) * 128]
            fin[b, 2 * m + 1 : 2 * m + 2, :] = second[:, b * 128 : (b + 1) * 128]

    def send_final(i, _):
        peer = lax.rem(me_b + 1 + i, N_BEAM)
        to_beam(fin.at[peer], fin_in.at[me_b], fin_send, fin_recv, peer).start()
        return 0

    lax.fori_loop(0, N_BEAM - 1, send_final, 0)

    def sent_grads(i, _):
        peer = far_z(i)
        to_z(gout.at[peer], gin.at[z], gr_send, gr_recv, peer).wait_send()
        return 0

    lax.fori_loop(0, 15, sent_grads, 0)

    def final_arrive(i, acc):
        source = lax.rem(me_b + N_BEAM - 1 - i, N_BEAM)
        came(fin_in.at[source], fin_send.at[source], fin_recv.at[source]).wait_recv()
        return acc + fin_in[source]

    result = lax.fori_loop(0, N_BEAM - 1, final_arrive, fin[me_b])
    out_ref[0] = result[0:2]
    out_ref[1] = result[2:4]

    def sent_final(i, _):
        peer = lax.rem(me_b + 1 + i, N_BEAM)
        to_beam(fin.at[peer], fin_in.at[me_b], fin_send, fin_recv, peer).wait_send()
        return 0

    lax.fori_loop(0, N_BEAM - 1, sent_final, 0)


def local(
    sky_harmonics,
    beam_harmonics,
    wigner,
    order_map,
    block_owner,
    block_local,
    cell_offset,
    cell_fraction,
    beam_angle,
    sample_count,
    noise_weight,
):
    hbm = pl.BlockSpec(memory_space=pl.ANY)
    vmem, smem, dma = pltpu.VMEM, pltpu.SMEM, pltpu.SemaphoreType.DMA
    owner = block_owner.reshape(NSB)
    return pl.pallas_call(
        kernel,
        out_shape=jax.ShapeDtypeStruct((2, 2, 128), F32),
        in_specs=[hbm] * 3 + [pl.BlockSpec(memory_space=smem)] + [hbm] * 9,
        out_specs=pl.BlockSpec(memory_space=pltpu.VMEM),
        scratch_shapes=[
            smem((NSB,), I32),
            smem((NSB,), I32),
            smem((64,), I32),
            vmem((1, NSB), I32),
            vmem((1, NSB), I32),
            vmem((2, 2, 2048), F32),
            vmem((KL, 2, 2048), F32),
            vmem((KL, 2, 64, 2048), BF16),
            vmem((NSB, 128), I32),
            vmem((NSB, 128), F32),
            vmem((NSB, 128), F32),
            vmem((128, 128), F32),
            vmem((128, 128), I32),
            vmem((PHI_BLOCKS, 128, 256), BF16),
            vmem((NSB, KL, 128), F32),
            vmem((NSB, 128, 128), BF16),
            vmem((16, 128), F32),
            vmem((16, 128), BF16),
            vmem((2, 16, 16, 128), BF16),
            vmem((512, 128), F32),
            vmem((64, KL, 128), F32),
            vmem((32, 128), F32),
            vmem((4, 32, 128), BF16),
            vmem((4, 4, 32, 128), BF16),
            vmem((4, 32, 128), BF16),
            vmem((4, 4, 32, 128), BF16),
            vmem((32, 128), F32),
            vmem((NSB * KL, 128), F32),
            vmem((512, 128), F32),
            vmem((256, 128), F32),
            vmem((16, 16, 128), BF16),
            vmem((16, 16, 128), BF16),
            vmem((N_BEAM, 4, 128), F32),
            vmem((N_BEAM, 4, 128), F32),
            dma((11,)),
            dma((4,)),
            dma((16,)),
            dma((16,)),
            dma,
            dma,
            dma((4, 4)),
            dma((4, 4)),
            dma((4, 4)),
            dma((4, 4)),
            dma,
            dma,
            dma((16,)),
            dma((16,)),
            dma((N_BEAM,)),
            dma((N_BEAM,)),
        ],
        compiler_params=pltpu.CompilerParams(collective_id=0, has_side_effects=True),
        name="normal_operator",
    )(
        owner,
        block_local,
        order_map,
        sample_count,
        owner.reshape(1, NSB),
        block_local.reshape(1, NSB),
        sky_harmonics,
        beam_harmonics,
        wigner,
        cell_offset.reshape(NSB, 128),
        cell_fraction.reshape(NSB, 128),
        beam_angle.reshape(NSB, 128),
        noise_weight,
    )


def solution(mesh):
    return jax.shard_map(
        local,
        mesh=mesh,
        in_specs=(
            P("ma", None, None),
            P("beam", None, None),
            P("beam", "ma", None, None),
            P(),
            P("ma", None),
            P("ma"),
            P("ma"),
            P("ma"),
            P("ma"),
            P("ma"),
            P(),
        ),
        out_specs=P("ma", None, "beam"),
        check_vma=False,
    )
```

time: 60.8 us -> 56 us (0.921)
  Pallas kernels: 58.7 us -> 53.9 us
    pallas_call x1, Pallas kernels: 58.7 us -> 53.9 us  [local(): pl.pallas_call(kernel, out_shape=jax.ShapeDtypeStruct((2, 2, 128), F32),...]
where the time goes in v2:
time: 56 us; the launch traced here: 55.8 us
  Pallas kernels  53.9 us (96%)
  local copies, waits for them, and re-layouts  1.26 us (2%)
  between operations  0.66 us (1%)
    pallas_call x1, Pallas kernels, local(): pl.pallas_call(kernel, out_shape=jax.ShapeDtypeStruct((2, 2, 128), F32),...  53.9 us
    unnamed x1, local copies, waits for them, and re-layouts  1.26 us

profile of v2, /device:TPU:1, one launch (start us, length us, event | category | flops | bytes accessed | tf_op | source)
XLA Modules:
  0.0 55.8 jit_solution(15120126168395763887)
XLA Ops:
  0.7 53.9 %normal_operator.1 = f32[2,2,128]{2,1,0:T(2,128)} custom-call(s32[128]{0:T(128)} %bitcast.9, s32[128]{0:T(128)} %local_hbm.1, s32[64]{0:T(128)} %order_hbm.1, s32[1]{0:T(128)S(6)} %copy.13.count_s, s32[1,128]{1,0:T(1,128)} %bitcast.10, s32[1,128]{1,0:T(1,128)} %bitcast.11, f32[2,2,2048]{2,1,0:T(2,128)} %sky_hbm.1, f32[8,2,2048]{2,1,0:T(2,128)} %beam_hbm.1, ...), custom_call_target="tpu_custom_call" | custom-call | tf_op jit(solution)/shard_map/normal_operator/pallas_call | solution.py:481
  54.6 1.3 %copy.14 = f32[2,2,128]{2,1,0:T(2,128)} copy(f32[2,2,128]{2,1,0:T(2,128)} %normal_operator.1) | data formatting | bytes 4096

commit v3 on v2

--- a/solution.py
+++ b/solution.py
@@ -26,6 +26,7 @@
 KL = 8
 PHI_BLOCKS = 32
 NSB = 128
+EARLY = 16
 
 
 def cos_turns(turns):
@@ -156,17 +157,22 @@
         half = (i + 1) // 2
         return lax.rem(z + 16 + 8 + half * (1 - 2 * lax.rem(i, 2)), 16)
 
-    def greet_z(i, _):
-        pl.semaphore_signal(barrier, inc=1, device_id={"ma": far_z(i) * 2 + core})
-        return 0
-
-    def greet_beam(i, _):
-        pl.semaphore_signal(barrier, inc=1, device_id={"beam": lax.rem(me_b + i, N_BEAM)})
-        return 0
-
+    def along_x(i):
+        return y * 4 + lax.rem(x + i, 4)
+
+    def along_y(i):
+        return lax.rem(y + i, 4) * 4 + x
+
+    def on_z(distance):
+        return lax.rem(z + 16 + distance, 16)
+
+    near = (4, -4, 3, -3, 2, -2, 1, -1)
     partner = z * 2 + 1 - core
-    lax.fori_loop(0, 15, greet_z, 0)
-    lax.fori_loop(1, N_BEAM, greet_beam, 0)
+    for distance in near:
+        pl.semaphore_signal(barrier, inc=1, device_id={"ma": on_z(distance) * 2 + core})
+    for i in (2, 1, 3):
+        pl.semaphore_signal(barrier, inc=1, device_id={"beam": along_x(i)})
+        pl.semaphore_signal(barrier, inc=1, device_id={"beam": along_y(i)})
     pl.semaphore_signal(barrier, inc=1, device_id={"ma": partner})
     for copy in loads[2:]:
         copy.start()
@@ -217,13 +223,19 @@
                     )
     piece[...] = rows[...].astype(BF16)
 
-    pl.semaphore_wait(barrier, 15 + 15 + 1)
-
-    def send_modes(i, _):
-        to_z(piece, gathered.at[core, z], ag_send, ag_recv, far_z(i)).start()
-        return 0
-
-    lax.fori_loop(0, 15, send_modes, 0)
+    pl.semaphore_wait(barrier, len(near) + 6 + 1)
+    sent_modes = []
+    for i, distance in enumerate(near):
+        sent_modes.append(
+            remote(
+                piece,
+                gathered.at[core, z],
+                ag_send.at[i],
+                ag_recv.at[z],
+                ma=on_z(distance) * 2 + core,
+            )
+        )
+        sent_modes[-1].start()
     gathered[core, z] = piece[...]
 
     for copy in loads[2:]:
@@ -257,24 +269,43 @@
 
     cell = lax.broadcasted_iota(I32, (128, 128), 0)
 
-    def interpolators(s, _):
+    def interpolator(s):
         block = lax.rem(local_s[s], PHI_BLOCKS)
         low = offset[pl.ds(s, 1), :]
         right = fraction[pl.ds(s, 1), :]
         mix = jnp.where(
             cell == low, 1.0 - right, jnp.where(cell == low + 1, right, 0.0)
         ).astype(BF16)
-        interp[s] = nn(phase[block], jnp.concatenate([mix, mix], axis=0)).astype(BF16)
+        return nn(phase[block], jnp.concatenate([mix, mix], axis=0)).astype(BF16)
+
+    def interpolator_pair(i, _):
+        interp[i] = jnp.concatenate([interpolator(2 * i), interpolator(2 * i + 1)], axis=1)
         return 0
 
-    lax.fori_loop(0, NSB, interpolators, 0, unroll=4)
-
-    def modes_arrive(i, _):
-        source = far_z(14 - i)
-        came(gathered.at[core, source], ag_send.at[source], ag_recv.at[source]).wait_recv()
-        return 0
-
-    lax.fori_loop(0, 15, modes_arrive, 0)
+    def modes_of(distance):
+        source = on_z(distance)
+        came(gathered.at[core, source], ag_send.at[0], ag_recv.at[source]).wait_recv()
+
+    lax.fori_loop(0, EARLY, interpolator_pair, 0, unroll=2)
+
+    for source, onward in ((-4, (4, 3, 2, 1)), (4, (-3, -2, -1))):
+        modes_of(source)
+        block = gathered.at[core, on_z(source)]
+        for distance in onward:
+            i = len(sent_modes)
+            sent_modes.append(
+                remote(
+                    block,
+                    block,
+                    ag_send.at[i],
+                    ag_recv.at[on_z(source)],
+                    ma=on_z(distance) * 2 + core,
+                )
+            )
+            sent_modes[-1].start()
+    lax.fori_loop(EARLY, NSB // 2, interpolator_pair, 0, unroll=2)
+    for distance in (3, -3, 2, -2, 1, -1, 5, -5, 6, -6, 7, -7, 8):
+        modes_of(distance)
     swap_modes = remote(gathered.at[core], gathered.at[core], agp_send, agp_recv, ma=partner)
     swap_modes.start()
     came(gathered.at[1 - core], agp_send, agp_recv).wait_recv()
@@ -285,19 +316,16 @@
         modes[:, 2 * kp + 1, :] = block[64:]
 
     def forward(first, rows_at):
-        for j in range(16):
-            s = first + j
-            cycle = owner_s[s] * 2 + lax.div(local_s[s], PHI_BLOCKS)
-            values = nn(modes[cycle].astype(BF16), interp[s])
-            partial[rows_at + j : rows_at + j + 1, :] = jnp.sum(
-                turn[s] * values, axis=0, keepdims=True
-            )
-
-    def along_x(i):
-        return y * 4 + lax.rem(x + i, 4)
-
-    def along_y(i):
-        return lax.rem(y + i, 4) * 4 + x
+        for j in range(0, 16, 2):
+            own = []
+            for s in (first + j, first + j + 1):
+                own.append(modes[owner_s[s] * 2 + lax.div(local_s[s], PHI_BLOCKS)])
+            values = nn(jnp.concatenate(own, axis=0).astype(BF16), interp[(first + j) // 2])
+            for i in range(2):
+                part = values[i * KL : (i + 1) * KL, i * 128 : (i + 1) * 128]
+                partial[rows_at + j + i : rows_at + j + i + 1, :] = jnp.sum(
+                    turn[first + j + i] * part, axis=0, keepdims=True
+                )
 
     def exchange(chunk, stage, out, into, send, recv):
         x_first = chunk < 2
@@ -344,11 +372,18 @@
             copy.start()
 
     def backward(first, rows_at):
-        for j in range(16):
+        for j in range(0, 16, 2):
+            lhs = []
+            for i in (j, j + 1):
+                lhs += split(turn[first + i] * filtered[rows_at + i : rows_at + i + 1, :])
+            weights = interp[(first + j) // 2]
+            weights = jnp.concatenate([weights[:, :128], weights[:, 128:]], axis=0)
+            both = nt(jnp.concatenate(lhs, axis=0), weights)
             s = first + j
-            high, low = split(turn[s] * filtered[rows_at + j : rows_at + j + 1, :])
-            both = nt(jnp.concatenate([high, low], axis=0), interp[s])
-            gmat[s * KL : (s + 1) * KL, :] = both[:KL] + both[KL:]
+            gmat[s * KL : (s + 1) * KL, :] = both[:KL, :128] + both[KL : 2 * KL, :128]
+            gmat[(s + 1) * KL : (s + 2) * KL, :] = (
+                both[2 * KL : 3 * KL, 128:] + both[3 * KL :, 128:]
+            )
 
     for chunk in sequence:
         signal = collect(chunk, 1, sum2_out[chunk].astype(F32), sum2_in, s2_send, s2_recv)
@@ -384,13 +419,8 @@
     swap_grads = remote(gout_f.at[pl.ds(other_rows, 256)], gpair, grp_send, grp_recv, ma=partner)
     swap_grads.start()
     swap_modes.wait_send()
-
-    def sent_modes(i, _):
-        peer = far_z(i)
-        to_z(piece, gathered.at[core, z], ag_send, ag_recv, peer).wait_send()
-        return 0
-
-    lax.fori_loop(0, 15, sent_modes, 0)
+    for copy in sent_modes:
+        copy.wait_send()
     came(gpair, grp_send, grp_recv).wait_recv()
     gout[...] = (gout_f[pl.ds(half_rows, 256), :] + gpair[...]).reshape(16, 16, 128).astype(BF16)
 
@@ -480,7 +510,7 @@
     owner = block_owner.reshape(NSB)
     return pl.pallas_call(
         kernel,
-        out_shape=jax.ShapeDtypeStruct((2, 2, 128), F32),
+        out_shape=pltpu.VMEM((2, 2, 128), F32),
         in_specs=[hbm] * 3 + [pl.BlockSpec(memory_space=smem)] + [hbm] * 9,
         out_specs=pl.BlockSpec(memory_space=pltpu.VMEM),
         scratch_shapes=[
@@ -499,7 +529,7 @@
             vmem((128, 128), I32),
             vmem((PHI_BLOCKS, 128, 256), BF16),
             vmem((NSB, KL, 128), F32),
-            vmem((NSB, 128, 128), BF16),
+            vmem((NSB // 2, 128, 256), BF16),
             vmem((16, 128), F32),
             vmem((16, 128), BF16),
             vmem((2, 16, 16, 128), BF16),

time: 56 us -> 52.7 us (0.941)
  Pallas kernels: 53.9 us -> 51.4 us
  local copies, waits for them, and re-layouts: 1.26 us -> 0.58 us
    pallas_call x1, Pallas kernels: 53.9 us -> 51.4 us  [local(): pl.pallas_call(kernel, out_shape=pltpu.VMEM((2, 2, 128), F32), in_specs=[...]
    unnamed x1, local copies, waits for them, and re-layouts: 1.26 us -> 0.58 us
where the time goes in v3:
time: 52.7 us; the launch traced here: 52.6 us
  Pallas kernels  51.4 us (98%)
  between operations  0.66 us (1%)
  local copies, waits for them, and re-layouts  0.58 us (1%)
    pallas_call x1, Pallas kernels, local(): pl.pallas_call(kernel, out_shape=pltpu.VMEM((2, 2, 128), F32), in_specs=[...  51.4 us

profile of v3, /device:TPU:1, one launch (start us, length us, event | category | flops | bytes accessed | tf_op | source)
XLA Modules:
  0.0 52.6 jit_solution(17472603969461555280)
XLA Ops:
  0.7 51.4 %normal_operator.1 = f32[2,2,128]{2,1,0:T(2,128)S(1)} custom-call(s32[128]{0:T(128)} %bitcast.9, s32[128]{0:T(128)} %local_hbm.1, s32[64]{0:T(128)} %order_hbm.1, s32[1]{0:T(128)S(6)} %copy.14.count_s, s32[1,128]{1,0:T(1,128)} %bitcast.10, s32[1,128]{1,0:T(1,128)} %bitcast.11, f32[2,2,2048]{2,1,0:T(2,128)} %sky_hbm.1, f32[8,2,2048]{2,1,0:T(2,128)} %beam_hbm.1, ...), custom_call_target="tpu_custom_call" | custom-call | tf_op jit(solution)/shard_map/normal_operator/pallas_call | solution.py:511
  52.0 0.6 %copy.13 = f32[2,2,128]{2,1,0:T(2,128)} copy(f32[2,2,128]{2,1,0:T(2,128)S(1)} %normal_operator.1) | data formatting | bytes 4096

commit v4 on v3

--- a/solution.py
+++ b/solution.py
@@ -128,10 +128,10 @@
         pltpu.make_async_copy(src, dst, load_sem.at[i])
         for i, (src, dst) in enumerate(
             [
+                (order_hbm, order_s),
+                (angle_hbm, angle),
                 (beam_hbm, beam),
                 (sky_hbm, sky),
-                (order_hbm, order_s),
-                (angle_hbm, angle),
                 (local_hbm, local_s),
                 (owner_hbm, owner_s),
                 (offset_hbm, offset),
@@ -146,9 +146,7 @@
         pltpu.make_async_copy(wig_hbm.at[pl.ds(2 * i, 2)], wig.at[pl.ds(2 * i, 2)], wig_sem.at[i])
         for i in range(4)
     ]
-    loads[0].start()
-    loads[1].start()
-    for copy in wig_loads:
+    for copy in loads[:4] + wig_loads + loads[4:]:
         copy.start()
 
     barrier = pltpu.get_barrier_semaphore()
@@ -174,8 +172,6 @@
         pl.semaphore_signal(barrier, inc=1, device_id={"beam": along_x(i)})
         pl.semaphore_signal(barrier, inc=1, device_id={"beam": along_y(i)})
     pl.semaphore_signal(barrier, inc=1, device_id={"ma": partner})
-    for copy in loads[2:]:
-        copy.start()
 
     def remote(src, dst, send, recv, **peer):
         return pltpu.make_async_remote_copy(
@@ -191,8 +187,50 @@
     def came(dst, send, recv):
         return remote(dst, dst, send, recv, ma=me_a)
 
+    sub = lax.broadcasted_iota(I32, (KL, 128), 0)
+    lane = lax.broadcasted_iota(I32, (KL, 128), 1)
+
     loads[0].wait()
+    for a_core in range(2):
+        for a_z in range(16):
+            for m in range(2):
+                row = (a_core * 16 + a_z) * 4 + m * 2
+                order[row : row + 2, :] = jnp.full((2, 128), order_s[(a_z * 2 + a_core) * 2 + m], I32)
+    for half in range(2):
+        orders = order[half * 64 : half * 64 + 64, :].astype(F32)
+        cells = lax.broadcasted_iota(I32, (64, 128), 1).astype(F32) * (1.0 / 4096.0)
+        quarter = (lax.broadcasted_iota(I32, (64, 128), 0) % 2).astype(F32) * 0.25
+        start = orders * cells + quarter
+        step = orders * (1.0 / 32.0)
+        step_re = cos_turns(step)
+        step_im = cos_turns(step - 0.25)
+
+        def phases(b, carried):
+            re, im = carried
+            phase[b, half * 64 : half * 64 + 64, :] = re.astype(BF16)
+            return re * step_re - im * step_im, im * step_re + re * step_im
+
+        lax.fori_loop(
+            0,
+            PHI_BLOCKS,
+            phases,
+            (cos_turns(start) * 0.125, cos_turns(start - 0.25) * 0.125),
+            unroll=2,
+        )
     loads[1].wait()
+    beam_order = me_b * KL + sub
+    spin = ((beam_order + 1) // 2).astype(F32)
+    back = (beam_order % 2).astype(F32) * 0.25
+
+    def turns_of(s, _):
+        around = angle[pl.ds(s, 1), :] * (1.0 / (2.0 * math.pi))
+        turn[s] = cos_turns(spin * around - back) * (1.0 / math.sqrt(128.0))
+        return 0
+
+    lax.fori_loop(0, NSB, turns_of, 0, unroll=4)
+
+    loads[2].wait()
+    loads[3].wait()
     beam_re = beam[:, 0, :]
     beam_im = beam[:, 1, :]
     products = []
@@ -204,8 +242,6 @@
                 [sky_re * beam_re - sky_im * beam_im, sky_re * beam_im + sky_im * beam_re], axis=0
             ).astype(BF16)
         )
-    sub = lax.broadcasted_iota(I32, (KL, 128), 0)
-    lane = lax.broadcasted_iota(I32, (KL, 128), 1)
     for quad in range(2):
         wig_loads[2 * quad].wait()
         wig_loads[2 * quad + 1].wait()
@@ -238,45 +274,23 @@
         sent_modes[-1].start()
     gathered[core, z] = piece[...]
 
-    for copy in loads[2:]:
+    for copy in loads[4:]:
         copy.wait()
-    for a_core in range(2):
-        for a_z in range(16):
-            for m in range(2):
-                row = (a_core * 16 + a_z) * 4 + m * 2
-                order[row : row + 2, :] = jnp.full((2, 128), order_s[(a_z * 2 + a_core) * 2 + m], I32)
-    quarter = (lax.broadcasted_iota(I32, (128, 128), 0) % 2).astype(F32) * 0.25
-
-    def phases(b, _):
-        cells = (b * 128 + lax.broadcasted_iota(I32, (128, 128), 1)).astype(F32) * (1.0 / 4096.0)
-        turns = order[...].astype(F32) * cells + quarter
-        high, low = split(cos_turns(turns) * 0.125)
-        phase[b] = jnp.concatenate([high, low], axis=1)
-        return 0
-
-    lax.fori_loop(0, PHI_BLOCKS, phases, 0)
-
-    beam_order = me_b * KL + sub
-    spin = ((beam_order + 1) // 2).astype(F32)
-    back = (beam_order % 2).astype(F32) * 0.25
-
-    def turns_of(s, _):
-        around = angle[pl.ds(s, 1), :] * (1.0 / (2.0 * math.pi))
-        turn[s] = cos_turns(spin * around - back) * (1.0 / math.sqrt(128.0))
-        return 0
-
-    lax.fori_loop(0, NSB, turns_of, 0, unroll=4)
-
-    cell = lax.broadcasted_iota(I32, (128, 128), 0)
+    cell = lax.broadcasted_iota(I32, (128, 128), 0).astype(F32).astype(BF16)
+
+    def spread(row):
+        return jnp.concatenate([jnp.broadcast_to(row, (16, 128)).astype(BF16)] * 8, axis=0)
 
     def interpolator(s):
         block = lax.rem(local_s[s], PHI_BLOCKS)
-        low = offset[pl.ds(s, 1), :]
+        away = cell - spread(offset[pl.ds(s, 1), :].astype(F32))
         right = fraction[pl.ds(s, 1), :]
         mix = jnp.where(
-            cell == low, 1.0 - right, jnp.where(cell == low + 1, right, 0.0)
-        ).astype(BF16)
-        return nn(phase[block], jnp.concatenate([mix, mix], axis=0)).astype(BF16)
+            away == 0.0,
+            spread(1.0 - right),
+            jnp.where(away == 1.0, spread(right), jnp.zeros((128, 128), BF16)),
+        )
+        return nn(phase[block], mix).astype(BF16)
 
     def interpolator_pair(i, _):
         interp[i] = jnp.concatenate([interpolator(2 * i), interpolator(2 * i + 1)], axis=1)
@@ -527,7 +541,7 @@
             vmem((NSB, 128), F32),
             vmem((128, 128), F32),
             vmem((128, 128), I32),
-            vmem((PHI_BLOCKS, 128, 256), BF16),
+            vmem((PHI_BLOCKS, 128, 128), BF16),
             vmem((NSB, KL, 128), F32),
             vmem((NSB // 2, 128, 256), BF16),
             vmem((16, 128), F32),

time: 52.7 us -> 50.6 us (0.960)
  Pallas kernels: 51.4 us -> 49.2 us
    pallas_call x1, Pallas kernels: 51.4 us -> 49.2 us  [local(): pl.pallas_call(kernel, out_shape=pltpu.VMEM((2, 2, 128), F32), in_specs=[...]
where the time goes in v4:
time: 50.6 us; the launch traced here: 50.5 us
  Pallas kernels  49.2 us (97%)
  between operations  0.66 us (1%)
  local copies, waits for them, and re-layouts  0.58 us (1%)
    pallas_call x1, Pallas kernels, local(): pl.pallas_call(kernel, out_shape=pltpu.VMEM((2, 2, 128), F32), in_specs=[...  49.2 us

profile of v4, /device:TPU:1, one launch (start us, length us, event | category | flops | bytes accessed | tf_op | source)
XLA Modules:
  0.0 50.5 jit_solution(1733541307856418406)
XLA Ops:
  0.7 49.2 %normal_operator.1 = f32[2,2,128]{2,1,0:T(2,128)S(1)} custom-call(s32[128]{0:T(128)} %bitcast.9, s32[128]{0:T(128)} %local_hbm.1, s32[64]{0:T(128)} %order_hbm.1, s32[1]{0:T(128)S(6)} %copy.14.count_s, s32[1,128]{1,0:T(1,128)} %bitcast.10, s32[1,128]{1,0:T(1,128)} %bitcast.11, f32[2,2,2048]{2,1,0:T(2,128)} %sky_hbm.1, f32[8,2,2048]{2,1,0:T(2,128)} %beam_hbm.1, ...), custom_call_target="tpu_custom_call" | custom-call | tf_op jit(solution)/shard_map/normal_operator/pallas_call | solution.py:525
  49.9 0.6 %copy.13 = f32[2,2,128]{2,1,0:T(2,128)} copy(f32[2,2,128]{2,1,0:T(2,128)S(1)} %normal_operator.1) | data formatting | bytes 4096

commit v5 on v4

--- a/solution.py
+++ b/solution.py
@@ -146,7 +146,7 @@
         pltpu.make_async_copy(wig_hbm.at[pl.ds(2 * i, 2)], wig.at[pl.ds(2 * i, 2)], wig_sem.at[i])
         for i in range(4)
     ]
-    for copy in loads[:4] + wig_loads + loads[4:]:
+    for copy in loads[:4] + wig_loads:
         copy.start()
 
     barrier = pltpu.get_barrier_semaphore()
@@ -172,6 +172,8 @@
         pl.semaphore_signal(barrier, inc=1, device_id={"beam": along_x(i)})
         pl.semaphore_signal(barrier, inc=1, device_id={"beam": along_y(i)})
     pl.semaphore_signal(barrier, inc=1, device_id={"ma": partner})
+    for copy in loads[4:]:
+        copy.start()
 
     def remote(src, dst, send, recv, **peer):
         return pltpu.make_async_remote_copy(
@@ -292,6 +294,9 @@
         )
         return nn(phase[block], mix).astype(BF16)
 
+    noise_high, noise_low = split(noise[...])
+    noise_twice = jnp.concatenate([noise_high, noise_high], axis=1)
+
     def interpolator_pair(i, _):
         interp[i] = jnp.concatenate([interpolator(2 * i), interpolator(2 * i + 1)], axis=1)
         return 0
@@ -342,7 +347,7 @@
                 )
 
     def exchange(chunk, stage, out, into, send, recv):
-        x_first = chunk < 2
+        x_first = chunk == 0
         use_x = x_first if stage == 0 else not x_first
         mine = x if use_x else y
         copies = []
@@ -360,7 +365,7 @@
         return copies
 
     def collect(chunk, stage, own, into, send, recv):
-        x_first = chunk < 2
+        x_first = chunk == 0
         use_x = x_first if stage == 0 else not x_first
         mine = x if use_x else y
         total = own
@@ -370,12 +375,12 @@
             total = total + into[chunk, source].astype(F32)
         return total
 
-    first_stage = [exchange(c, 0, sum_out, sum_in, s1_send, s1_recv) for c in range(4)]
-    second_stage = [exchange(c, 1, sum2_out, sum2_in, s2_send, s2_recv) for c in range(4)]
-    sequence = (0, 2, 1, 3)
+    first_stage = [exchange(c, 0, sum_out, sum_in, s1_send, s1_recv) for c in range(2)]
+    second_stage = [exchange(c, 1, sum2_out, sum2_in, s2_send, s2_recv) for c in range(2)]
+    sequence = (0, 1)
     for chunk in sequence:
-        forward(chunk * 32, 0)
-        forward(chunk * 32 + 16, 16)
+        for rows_at in range(0, 64, 16):
+            forward(chunk * 64 + rows_at, rows_at)
         sum_out[chunk] = partial[...].astype(BF16)
         for copy in first_stage[chunk]:
             copy.start()
@@ -389,34 +394,25 @@
         for j in range(0, 16, 2):
             lhs = []
             for i in (j, j + 1):
-                lhs += split(turn[first + i] * filtered[rows_at + i : rows_at + i + 1, :])
+                lhs.append(turn[first + i] * filtered[rows_at + i : rows_at + i + 1, :])
             weights = interp[(first + j) // 2]
             weights = jnp.concatenate([weights[:, :128], weights[:, 128:]], axis=0)
-            both = nt(jnp.concatenate(lhs, axis=0), weights)
+            both = nt(jnp.concatenate(lhs, axis=0).astype(BF16), weights)
             s = first + j
-            gmat[s * KL : (s + 1) * KL, :] = both[:KL, :128] + both[KL : 2 * KL, :128]
-            gmat[(s + 1) * KL : (s + 2) * KL, :] = (
-                both[2 * KL : 3 * KL, 128:] + both[3 * KL :, 128:]
-            )
+            gmat[s * KL : (s + 1) * KL, :] = both[:KL, :128]
+            gmat[(s + 1) * KL : (s + 2) * KL, :] = both[KL:, 128:]
 
     for chunk in sequence:
         signal = collect(chunk, 1, sum2_out[chunk].astype(F32), sum2_in, s2_send, s2_recv)
         stamps = (
-            chunk * 32 + lax.broadcasted_iota(I32, (32, 128), 0)
-        ) * 128 + lax.broadcasted_iota(I32, (32, 128), 1)
+            chunk * 64 + lax.broadcasted_iota(I32, (64, 128), 0)
+        ) * 128 + lax.broadcasted_iota(I32, (64, 128), 1)
         valid = (stamps < count_s[0]).astype(F32)
-        filtered[...] = (
-            lax.dot_general(
-                signal * valid,
-                noise[...],
-                (((1,), (1,)), ((), ())),
-                precision=lax.Precision.HIGHEST,
-                preferred_element_type=F32,
-            )
-            * valid
-        )
-        backward(chunk * 32, 0)
-        backward(chunk * 32 + 16, 16)
+        high, low = split(signal * valid)
+        mixed = nt(jnp.concatenate([high, low], axis=1), noise_twice) + nt(high, noise_low)
+        filtered[...] = mixed * valid
+        for rows_at in range(0, 64, 16):
+            backward(chunk * 64 + rows_at, rows_at)
 
     cycles = owner_row[...] * 2 + lax.div(local_row[...], jnp.full((1, NSB), PHI_BLOCKS, I32))
     pick = (lax.broadcasted_iota(I32, (64, 128), 0) == cycles).astype(F32).astype(BF16)
@@ -444,7 +440,7 @@
         return 0
 
     lax.fori_loop(0, 15, send_grads, 0)
-    for chunk in range(4):
+    for chunk in range(2):
         for copy in first_stage[chunk] + second_stage[chunk]:
             copy.wait_send()
     swap_grads.wait_send()
@@ -549,12 +545,12 @@
             vmem((2, 16, 16, 128), BF16),
             vmem((512, 128), F32),
             vmem((64, KL, 128), F32),
-            vmem((32, 128), F32),
-            vmem((4, 32, 128), BF16),
-            vmem((4, 4, 32, 128), BF16),
-            vmem((4, 32, 128), BF16),
-            vmem((4, 4, 32, 128), BF16),
-            vmem((32, 128), F32),
+            vmem((64, 128), F32),
+            vmem((2, 64, 128), BF16),
+            vmem((2, 4, 64, 128), BF16),
+            vmem((2, 64, 128), BF16),
+            vmem((2, 4, 64, 128), BF16),
+            vmem((64, 128), F32),
             vmem((NSB * KL, 128), F32),
             vmem((512, 128), F32),
             vmem((256, 128), F32),
@@ -568,10 +564,10 @@
             dma((16,)),
             dma,
             dma,
-            dma((4, 4)),
-            dma((4, 4)),
-            dma((4, 4)),
-            dma((4, 4)),
+            dma((2, 4)),
+            dma((2, 4)),
+            dma((2, 4)),
+            dma((2, 4)),
             dma,
             dma,
             dma((16,)),

time: 50.6 us -> 49.3 us (0.974)
  Pallas kernels: 49.2 us -> 47.9 us
    pallas_call x1, Pallas kernels: 49.2 us -> 47.9 us  [local(): pl.pallas_call(kernel, out_shape=pltpu.VMEM((2, 2, 128), F32), in_specs=[...]
where the time goes in v5:
time: 49.3 us; the launch traced here: 49.2 us
  Pallas kernels  47.9 us (97%)
  between operations  0.66 us (1%)
  local copies, waits for them, and re-layouts  0.58 us (1%)
    pallas_call x1, Pallas kernels, local(): pl.pallas_call(kernel, out_shape=pltpu.VMEM((2, 2, 128), F32), in_specs=[...  47.9 us

profile of v5, /device:TPU:1, one launch (start us, length us, event | category | flops | bytes accessed | tf_op | source)
XLA Modules:
  0.0 49.2 jit_solution(17626831197321454731)
XLA Ops:
  0.7 47.9 %normal_operator.1 = f32[2,2,128]{2,1,0:T(2,128)S(1)} custom-call(s32[128]{0:T(128)} %bitcast.9, s32[128]{0:T(128)} %local_hbm.1, s32[64]{0:T(128)} %order_hbm.1, s32[1]{0:T(128)S(6)} %copy.14.count_s, s32[1,128]{1,0:T(1,128)} %bitcast.10, s32[1,128]{1,0:T(1,128)} %bitcast.11, f32[2,2,2048]{2,1,0:T(2,128)} %sky_hbm.1, f32[8,2,2048]{2,1,0:T(2,128)} %beam_hbm.1, ...), custom_call_target="tpu_custom_call" | custom-call | tf_op jit(solution)/shard_map/normal_operator/pallas_call | solution.py:521
  48.6 0.6 %copy.13 = f32[2,2,128]{2,1,0:T(2,128)} copy(f32[2,2,128]{2,1,0:T(2,128)S(1)} %normal_operator.1) | data formatting | bytes 4096

commit v6 on v5

--- a/solution.py
+++ b/solution.py
@@ -434,12 +434,9 @@
     came(gpair, grp_send, grp_recv).wait_recv()
     gout[...] = (gout_f[pl.ds(half_rows, 256), :] + gpair[...]).reshape(16, 16, 128).astype(BF16)
 
-    def send_grads(i, _):
-        peer = far_z(i)
+    for distance in (8, 7, -7, 6, -6, 5, -5, 4, -4, 3, -3, 2, -2, 1, -1):
+        peer = on_z(distance)
         to_z(gout.at[peer], gin.at[z], gr_send, gr_recv, peer).start()
-        return 0
-
-    lax.fori_loop(0, 15, send_grads, 0)
     for chunk in range(2):
         for copy in first_stage[chunk] + second_stage[chunk]:
             copy.wait_send()
@@ -471,12 +468,15 @@
             fin[b, 2 * m : 2 * m + 1, :] = first[:, b * 128 : (b + 1) * 128]
             fin[b, 2 * m + 1 : 2 * m + 2, :] = second[:, b * 128 : (b + 1) * 128]
 
-    def send_final(i, _):
-        peer = lax.rem(me_b + 1 + i, N_BEAM)
-        to_beam(fin.at[peer], fin_in.at[me_b], fin_send, fin_recv, peer).start()
-        return 0
-
-    lax.fori_loop(0, N_BEAM - 1, send_final, 0)
+    steps = sorted(
+        ((dx, dy) for dx in range(4) for dy in range(4) if dx or dy),
+        key=lambda d: -(min(d[0], 4 - d[0]) + min(d[1], 4 - d[1])),
+    )
+    final_copies = []
+    for dx, dy in steps:
+        peer = lax.rem(y + dy, 4) * 4 + lax.rem(x + dx, 4)
+        final_copies.append(to_beam(fin.at[peer], fin_in.at[me_b], fin_send, fin_recv, peer))
+        final_copies[-1].start()
 
     def sent_grads(i, _):
         peer = far_z(i)
@@ -485,6 +485,9 @@
 
     lax.fori_loop(0, 15, sent_grads, 0)
 
+    for copy in final_copies:
+        copy.wait_send()
+
     def final_arrive(i, acc):
         source = lax.rem(me_b + N_BEAM - 1 - i, N_BEAM)
         came(fin_in.at[source], fin_send.at[source], fin_recv.at[source]).wait_recv()
@@ -493,13 +496,6 @@
     result = lax.fori_loop(0, N_BEAM - 1, final_arrive, fin[me_b])
     out_ref[0] = result[0:2]
     out_ref[1] = result[2:4]
-
-    def sent_final(i, _):
-        peer = lax.rem(me_b + 1 + i, N_BEAM)
-        to_beam(fin.at[peer], fin_in.at[me_b], fin_send, fin_recv, peer).wait_send()
-        return 0
-
-    lax.fori_loop(0, N_BEAM - 1, sent_final, 0)
 
 
 def local(

time: 49.3 us -> 49 us (level)
  no operation moved by 1% of the time
where the time goes in v6:
time: 49 us; the launch traced here: 48.9 us
  Pallas kernels  47.7 us (97%)
  between operations  0.66 us (1%)
  local copies, waits for them, and re-layouts  0.58 us (1%)
    pallas_call x1, Pallas kernels, local(): pl.pallas_call(kernel, out_shape=pltpu.VMEM((2, 2, 128), F32), in_specs=[...  47.7 us

profile of v6, /device:TPU:1, one launch (start us, length us, event | category | flops | bytes accessed | tf_op | source)
XLA Modules:
  0.0 48.9 jit_solution(18258420446659891644)
XLA Ops:
  0.7 47.7 %normal_operator.1 = f32[2,2,128]{2,1,0:T(2,128)S(1)} custom-call(s32[128]{0:T(128)} %bitcast.9, s32[128]{0:T(128)} %local_hbm.1, s32[64]{0:T(128)} %order_hbm.1, s32[1]{0:T(128)S(6)} %copy.14.count_s, s32[1,128]{1,0:T(1,128)} %bitcast.10, s32[1,128]{1,0:T(1,128)} %bitcast.11, f32[2,2,2048]{2,1,0:T(2,128)} %sky_hbm.1, f32[8,2,2048]{2,1,0:T(2,128)} %beam_hbm.1, ...), custom_call_target="tpu_custom_call" | custom-call | tf_op jit(solution)/shard_map/normal_operator/pallas_call | solution.py:517
  48.3 0.6 %copy.13 = f32[2,2,128]{2,1,0:T(2,128)} copy(f32[2,2,128]{2,1,0:T(2,128)S(1)} %normal_operator.1) | data formatting | bytes 4096
